TPU v7x, 256 devices: a whole 4x4x8 slice. The times are simulated.
256 devices in a mesh: facet: 16 (over z_hi, x, core), col: 16 (over y, z_lo).
Axes of the slice: x: 4, y: 4, z: 8 (z_hi: 2, z_lo: 4; z = z_hi * 4 + z_lo), core: 2. Of those that a mesh axis runs over, the one named last changes fastest.
Arguments:
- facet_spectra: bfloat16 [2, 16, 2, 512, 16384], P(None, 'facet', None, None, 'col'), may hold values from -6 to 6
- facet_offsets: int32 [16, 2], P('facet'), may hold values from 0 to 65535
- column_index: int32 [2], replicated, may hold values from 0 to 145
- subgrid_offsets: int32 [2, 16], P(None, 'col'), may hold values from 0 to 65532, as said below
- weights: bfloat16 [2, 16, 512, 512], P(None, 'col', 'facet'), may hold values from 0.25 to 4
Outputs:
- subgrids: bfloat16 [2, 16, 2, 512, 512], P(None, 'col', None, 'facet')
- facet_updates: bfloat16 [2, 16, 2, 512, 16384], P(None, 'facet', None, None, 'col')
Inputs may be any that keep to these rules, and one draw needn't show every extreme that they name: `subgrid_offsets`: every offset is a multiple of 4; subgrid s of a column has position p = offset / 4 with (s // 1) * 1024 <= p < (s + 1) * 1024. In every column some subgrid has p exactly at such a lower end, and some subgrid has p at (s + 1) * 1024 - 128 // 2 + 1 or above.
All inputs are finite; a program needn't handle non-finite values.
Results may differ from a plain program's by a relative error of at most 0.015.
Values may be sent and summed in bfloat16 or wider, within the bound.
A program may use at most 64 MiB of HBM per device.

v0:
```python
import math

import jax
import jax.numpy as jnp
from jax import lax
from jax.sharding import PartitionSpec as P

IMAGE = 65536
XM = 512
WM = 128
XA = 448


TAU = 2.0 * math.pi


def extended(block, sides, width):
    for axis, dim in sides:
        count = lax.axis_size(axis)
        forward = [(i, i + 1) for i in range(count - 1)]
        forward.append((count - 1, 0))
        backward = [(target, source) for source, target in forward]
        low = lax.ppermute(
            lax.slice_in_dim(block, block.shape[dim] - width, None, axis=dim), axis, forward
        )
        high = lax.ppermute(lax.slice_in_dim(block, 0, width, axis=dim), axis, backward)
        block = jnp.concatenate([low, block, high], axis=dim)
    return block


def split_up(array, dim, devices):
    before, after = (array.shape[:dim], array.shape[dim + 1 :])
    return jnp.moveaxis(array.reshape(*before, devices, -1, *after), dim, 0)


def sum_at_owner(array, axis, dim):
    devices = lax.axis_size(axis)
    tiles = lax.all_to_all(split_up(array, dim, devices), axis, 0, 0, tiled=True)
    return jnp.sum(tiles.astype(jnp.float32), axis=0)


def copy_for_each(array, axis):
    devices = lax.axis_size(axis)
    return lax.all_to_all(
        jnp.broadcast_to(array[None], (devices, *array.shape)), axis, 0, 0, tiled=True
    )


def in_order(tiles, dim):
    dims = list(tiles.shape[1:])
    dims[dim] *= tiles.shape[0]
    return jnp.moveaxis(tiles, 0, dim).reshape(dims)


def gather_directly(array, axis, dim):
    tiles = copy_for_each(array, axis)
    return in_order(tiles, dim)


def passed_along(block, axis, distance):
    devices = range(lax.axis_size(axis))
    route = [((i - distance) % len(devices), i) for i in devices]
    return lax.ppermute(block, axis, route)


def modular(first, second, image):
    upper = second // 256
    lower = second % 256
    return (first * upper % (image // 256) * 256 + first * lower) % image


def make_table(facets):
    place = jnp.arange(WM, dtype=jnp.int32)
    cell = jnp.arange(XM, dtype=jnp.int32)
    turns = (place[:, None] - WM // 2) * (cell[None, :] - XM // 2) % XM
    angle = TAU * turns.astype(jnp.float32) / XM
    relative = (place.astype(jnp.float32) + 0.5 - WM / 2.0) / (WM / 2.0)
    taper = (0.3 + 0.7 * (1.0 - relative * relative)) / jnp.sqrt(jnp.float32(WM * facets))
    return (
        (taper[:, None] * jnp.cos(angle)).astype(jnp.bfloat16),
        (taper[:, None] * jnp.sin(angle)).astype(jnp.bfloat16),
    )


def phases(column_pos, offsets, indices, length):
    first = modular(column_pos, offsets[0], IMAGE)
    second = indices * offsets[1] % length
    return TAU * (first.astype(jnp.float32) / IMAGE + second.astype(jnp.float32) / length)


def per_device(facet_spectra, facet_offsets, column_index, subgrid_offsets, weights):
    spectra = facet_spectra[:, 0]
    cols = spectra.shape[0]
    shard = spectra.shape[3]
    half = WM // 2
    facets = lax.axis_size("facet")
    length = shard * lax.axis_size("col")
    here = lax.axis_index("col")
    offsets = facet_offsets[0]
    real_tab, imag_tab = make_table(facets)
    padded = extended(spectra, (("col", 3),), half)
    grids = []
    buffers = []
    for column in range(cols):
        centres = subgrid_offsets[column] // (IMAGE // length)
        starts = centres - here * shard
        indices = (centres[:, None] - half + jnp.arange(WM, dtype=jnp.int32)[None, :]) % length
        column_pos = column_index[column] * XA
        angle = phases(column_pos, offsets, indices, length)
        cosine = jnp.cos(angle)
        sine = jnp.sin(angle)
        windows = jnp.stack([lax.dynamic_slice_in_dim(padded[column], starts[0], WM, 2)], axis=2)
        window = windows.astype(jnp.float32)
        phased_real = (window[0] * cosine + window[1] * sine).astype(jnp.bfloat16)
        phased_imag = (window[1] * cosine - window[0] * sine).astype(jnp.bfloat16)
        phased = jnp.stack([phased_real, phased_imag]).astype(jnp.float32)
        summed = sum_at_owner(phased.astype(jnp.bfloat16), "facet", 1)
        real_hi = real_tab.astype(jnp.float32)
        imag_hi = imag_tab.astype(jnp.float32)
        grid_real = jnp.einsum(
            "xsm,ml->sxl", summed[0], real_hi, precision=lax.Precision.HIGHEST
        ) - jnp.einsum("xsm,ml->sxl", summed[1], imag_hi, precision=lax.Precision.HIGHEST)
        grid_imag = jnp.einsum(
            "xsm,ml->sxl", summed[0], imag_hi, precision=lax.Precision.HIGHEST
        ) + jnp.einsum("xsm,ml->sxl", summed[1], real_hi, precision=lax.Precision.HIGHEST)
        grid = jnp.stack([grid_real, grid_imag], axis=1).astype(jnp.bfloat16)
        grids.append(grid)
        scaled = (grid.astype(jnp.float32) * weights[column].astype(jnp.float32)[:, None]).astype(
            jnp.bfloat16
        )
        back_real = jnp.einsum(
            "sxl,ml->sxm", scaled[:, 0], real_tab, preferred_element_type=jnp.float32
        ) + jnp.einsum("sxl,ml->sxm", scaled[:, 1], imag_tab, preferred_element_type=jnp.float32)
        back_imag = jnp.einsum(
            "sxl,ml->sxm", scaled[:, 1], real_tab, preferred_element_type=jnp.float32
        ) - jnp.einsum("sxl,ml->sxm", scaled[:, 0], imag_tab, preferred_element_type=jnp.float32)
        projected = gather_directly(jnp.stack([back_real, back_imag], axis=1), "facet", 2)
        upd_real = projected[:, 0] * cosine[:, None, :] - projected[:, 1] * sine[:, None, :]
        upd_imag = projected[:, 1] * cosine[:, None, :] + projected[:, 0] * sine[:, None, :]
        buffer = jnp.zeros((2, XM, shard + WM), jnp.float32)
        update = jnp.stack([upd_real[0], upd_imag[0]])
        buffer = lax.dynamic_update_slice_in_dim(buffer, update, starts[0], 2)
        buffers.append(buffer)
    stacked = jnp.stack(buffers)
    lower_part = stacked[..., :half]
    upper_part = stacked[..., shard + half :]
    middle = stacked[..., half : shard + half]
    from_below = passed_along(upper_part.astype(jnp.bfloat16), "col", 1).astype(upper_part.dtype)
    from_above = passed_along(lower_part.astype(jnp.bfloat16), "col", -1).astype(lower_part.dtype)
    middle = middle.at[..., :half].add(from_below)
    middle = middle.at[..., shard - half :].add(from_above)
    return (jnp.stack(grids), middle.astype(jnp.bfloat16)[:, None])


def solution(mesh):
    in_specs = (
        P(None, "facet", None, None, "col"),
        P("facet", None),
        P(),
        P(None, "col"),
        P(None, "col", "facet", None),
    )
    out_specs = (P(None, "col", None, "facet", None), P(None, "facet", None, None, "col"))
    return jax.shard_map(
        per_device, mesh=mesh, in_specs=in_specs, out_specs=out_specs, check_vma=False
    )
```

profile of v0, /device:TPU:1, one launch (start us, length us, event | category | flops | bytes accessed | tf_op | source)
XLA Modules:
  0.0 206.8 jit_solution(17852421410445415312)
XLA Ops:
  0.6 1.4 fusion.107
  2.1 7.7 %collective-permute-start.1 = (bf16[2,2,512,64]{3,2,1,0:T(8,128)(2,1)S(1)}, bf16[2,2,512,64]{3,2,1,0:T(8,128)(2,1)S(1)}, u32[]{:S(2)}, u32[]{:S(2)}) collective-permute-start(bf16[2,2,512,64]{3,2,1,0:T(8,128)(2,1)S(1)} %get-tuple-element.30), channel_id=1, source_target_pairs={{1,0},{2,1},{3,2},{4,3},{5,4},{6,5},{7,6},{8,7},{9,8},{10,9},{11,1... | collective-permute-start | bytes 786440 | tf_op jit(solution)/shard_map/ppermute | solution.py:26
  9.8 0.0 collective-permute-start
  9.8 1.4 fusion.110
  13.8 1.3 fusion.108
  16.4 1.3 fusion.109
  23.0 0.7 fusion.103
  23.7 0.8 fusion.101
  24.5 0.8 bitcast_convert_fusion
  25.3 0.0 collective-permute-done.1
  25.3 7.2 %collective-permute-done = bf16[2,2,512,64]{3,2,1,0:T(8,128)(2,1)S(1)} collective-permute-done((bf16[2,2,512,64]{3,2,1,0:T(8,128)(2,1)S(1)}, bf16[2,2,512,64]{3,2,1,0:T(8,128)(2,1)S(1)}, u32[]{:S(2)}, u32[]{:S(2)}) %collective-permute-start) | collective-permute-done | bytes 262176 | tf_op jit(solution)/shard_map/ppermute | solution.py:23
  32.5 9.2 %concatenate.45 = bf16[2,2,512,1152]{3,2,1,0:T(8,128)(2,1)} concatenate(bf16[2,2,512,64]{3,2,1,0:T(8,128)(2,1)S(1)} %collective-permute-done, bf16[2,2,512,1024]{3,2,1,0:T(8,128)(2,1)} %bitcast.161, bf16[2,2,512,64]{3,2,1,0:T(8,128)(2,1)S(1)} %collective-permute-done.1), dimensions={3} | concatenate | bytes 9437184 | tf_op jit(solution)/shard_map/concatenate | solution.py:27
  41.8 2.7 %fusion.106 = (bf16[1,2,512,1152]{3,2,1,0:T(8,128)(2,1)S(1)}, bf16[1,2,512,1152]{3,2,1,0:T(8,128)(2,1)S(1)}) fusion(bf16[2,2,512,1152]{3,2,1,0:T(8,128)(2,1)} %concatenate.45), kind=kLoop, calls=%fused_computation.182 | loop fusion | bytes 9437184 | tf_op jit(solution)/shard_map/slice | solution.py:112
  44.5 0.2 dynamic-slice_convert_fusion
  44.7 0.1 add_convert_fusion
  44.8 0.7 maximum_bitcast_fusion.3
  45.5 10.3 %all-to-all-start.1 = ((bf16[16,2,32,1,128]{4,2,3,1,0:T(8,128)(2,1)}), bf16[16,2,32,1,128]{4,2,3,1,0:T(8,128)(2,1)S(1)}, u32[]{:S(2)}, u32[]{:S(2)}) async-start(bf16[16,2,32,1,128]{4,2,3,1,0:T(8,128)(2,1)} %maximum_bitcast_fusion.3), calls=%async_computation.1 | async-start | bytes 524288 | tf_op jit(solution)/shard_map/all_to_all | solution.py:38
  55.9 0.1 add_convert_fusion.1
  56.0 0.7 maximum_bitcast_fusion.2
  56.7 10.3 %all-to-all-done.1 = bf16[16,2,32,1,128]{4,2,3,1,0:T(8,128)(2,1)S(1)} async-done(((bf16[16,2,32,1,128]{4,2,3,1,0:T(8,128)(2,1)}), bf16[16,2,32,1,128]{4,2,3,1,0:T(8,128)(2,1)S(1)}, u32[]{:S(2)}, u32[]{:S(2)}) %all-to-all-start.1) | async-done | bytes 262176 | tf_op jit(solution)/shard_map/all_to_all | solution.py:38
  67.0 5.9 %all-to-all-start = ((bf16[16,2,32,1,128]{4,2,3,1,0:T(8,128)(2,1)}), bf16[16,2,32,1,128]{4,2,3,1,0:T(8,128)(2,1)S(1)}, u32[]{:S(2)}, u32[]{:S(2)}) async-start(bf16[16,2,32,1,128]{4,2,3,1,0:T(8,128)(2,1)} %maximum_bitcast_fusion.2), calls=%async_computation | async-start | bytes 524288 | tf_op jit(solution)/shard_map/all_to_all | solution.py:38
  72.9 1.2 fusion.15
  74.1 1.2 fusion.21
  75.3 8.7 %all-to-all-done = bf16[16,2,32,1,128]{4,2,3,1,0:T(8,128)(2,1)S(1)} async-done(((bf16[16,2,32,1,128]{4,2,3,1,0:T(8,128)(2,1)}), bf16[16,2,32,1,128]{4,2,3,1,0:T(8,128)(2,1)S(1)}, u32[]{:S(2)}, u32[]{:S(2)}) %all-to-all-start) | async-done | bytes 262176 | tf_op jit(solution)/shard_map/all_to_all | solution.py:38
  84.0 1.2 fusion.16
  85.2 1.2 fusion.22
  86.4 1.2 fusion.3
  87.6 1.2 fusion.2
  88.9 1.1 fusion.19
  90.0 1.2 fusion.20
  91.2 1.2 fusion.5
  92.4 1.2 fusion.4
  93.6 1.4 fusion.8
  95.0 1.2 fusion.9
  96.2 0.9 broadcast_in_dim.11
  97.0 6.2 %all-to-all-start.2 = ((f32[16,1,2,32,128]{4,3,2,1,0:T(8,128)}), f32[16,1,2,32,128]{4,3,2,1,0:T(8,128)S(1)}, u32[]{:S(2)}, u32[]{:S(2)}) async-start(f32[16,1,2,32,128]{4,3,2,1,0:T(8,128)} %broadcast_in_dim.11), calls=%async_computation.2 | async-start | bytes 1048576 | tf_op jit(solution)/shard_map/all_to_all | solution.py:44
  103.3 1.1 fusion.17
  104.4 1.2 fusion.6
  105.6 1.1 fusion.18
  106.8 1.2 fusion.7
  108.0 8.9 %all-to-all-done.2 = f32[16,1,2,32,128]{4,3,2,1,0:T(8,128)S(1)} async-done(((f32[16,1,2,32,128]{4,3,2,1,0:T(8,128)}), f32[16,1,2,32,128]{4,3,2,1,0:T(8,128)S(1)}, u32[]{:S(2)}, u32[]{:S(2)}) %all-to-all-start.2) | async-done | bytes 524320 | tf_op jit(solution)/shard_map/all_to_all | solution.py:44
  116.8 0.9 broadcast_in_dim.13
  117.7 7.6 %all-to-all-start.3 = ((f32[16,1,2,32,128]{4,3,2,1,0:T(8,128)}), f32[16,1,2,32,128]{4,3,2,1,0:T(8,128)S(1)}, u32[]{:S(2)}, u32[]{:S(2)}) async-start(f32[16,1,2,32,128]{4,3,2,1,0:T(8,128)} %broadcast_in_dim.13), calls=%async_computation.3 | async-start | bytes 1048576 | tf_op jit(solution)/shard_map/all_to_all | solution.py:44
  125.3 0.7 maximum_maximum_fusion
  126.0 0.1 multiply_subtract_fusion.1
  126.1 12.8 %all-to-all-done.3 = f32[16,1,2,32,128]{4,3,2,1,0:T(8,128)S(1)} async-done(((f32[16,1,2,32,128]{4,3,2,1,0:T(8,128)}), f32[16,1,2,32,128]{4,3,2,1,0:T(8,128)S(1)}, u32[]{:S(2)}, u32[]{:S(2)}) %all-to-all-start.3) | async-done | bytes 524320 | tf_op jit(solution)/shard_map/all_to_all | solution.py:44
  138.9 0.1 multiply_subtract_fusion
  139.1 2.5 %stack.103.clone = f32[1,2,512,1152]{3,2,1,0:T(8,128)} broadcast(f32[]{:T(128)} %constant.243.clone.1), dimensions={} | broadcast | bytes 4718596 | tf_op jit(solution)/shard_map/stack | solution.py:144
  141.5 3.4 %dynamic_update_slice.8 = f32[1,2,512,1152]{3,2,1,0:T(8,128)} dynamic-update-slice(f32[1,2,512,1152]{3,2,1,0:T(8,128)} %stack.103.clone, f32[1,2,512,128]{3,2,1,0:T(8,128)S(1)} %maximum_bitcast_fusion, s32[]{:T(128)} %constant.217.clone.1, s32[]{:T(128)} %constant.217.clone.1, s32[]{:T(128)} %constant.217.clone.1, s32[]{:T(128)S(6)} %select_n.142) | dynamic-update-slice | bytes 1048580 | tf_op jit(solution)/shard_map/dynamic_update_slice | solution.py:142
  145.0 2.5 %stack.103.clone.1 = f32[1,2,512,1152]{3,2,1,0:T(8,128)} broadcast(f32[]{:T(128)} %constant.243.clone.1), dimensions={} | broadcast | bytes 4718596 | tf_op jit(solution)/shard_map/stack | solution.py:144
  147.5 3.9 %dynamic_update_slice.9 = f32[1,2,512,1152]{3,2,1,0:T(8,128)} dynamic-update-slice(f32[1,2,512,1152]{3,2,1,0:T(8,128)} %stack.103.clone.1, f32[1,2,512,128]{3,2,1,0:T(8,128)S(1)} %maximum_bitcast_fusion.1, s32[]{:T(128)} %constant.217.clone.1, s32[]{:T(128)} %constant.217.clone.1, s32[]{:T(128)} %constant.217.clone.1, s32[]{:T(128)S(6)} %select_n.150) | dynamic-update-slice | bytes 1048580 | tf_op jit(solution)/shard_map/dynamic_update_slice | solution.py:142
  151.4 4.6 %fusion = bf16[2,2,512,1152]{3,2,1,0:T(8,128)(2,1)S(1)} fusion(f32[1,2,512,1152]{3,2,1,0:T(8,128)} %dynamic_update_slice.9, f32[1,2,512,1152]{3,2,1,0:T(8,128)} %dynamic_update_slice.8), kind=kLoop, calls=%fused_computation.5 | loop fusion | flops 2359296 | bytes 14155776 | tf_op jit(solution)/shard_map/convert.3
  156.0 0.2 fusion.105
  156.3 0.1 collective-permute-start.3
  156.3 4.4 %collective-permute-start.2 = (bf16[2,2,512,64]{3,2,1,0:T(8,128)(2,1)S(1)}, bf16[2,2,512,64]{3,2,1,0:T(8,128)(2,1)S(1)}, u32[]{:S(2)}, u32[]{:S(2)}) collective-permute-start(bf16[2,2,512,64]{3,2,1,0:T(8,128)(2,1)S(1)} %get-tuple-element.27), channel_id=1, source_target_pairs={{15,0},{0,1},{1,2},{2,3},{3,4},{4,5},{5,6},{6,7},{7,8},{8,9},{9,10... | collective-permute-start | bytes 786440 | tf_op jit(solution)/shard_map/ppermute | solution.py:63
  160.8 0.0 slice-done.1
  160.8 5.1 %fusion.1 = f32[2,2,512,1024]{3,2,1,0:T(8,128)} fusion(f32[1,2,512,1152]{3,2,1,0:T(8,128)S(1)} %bitcast.159, f32[1,2,512,1152]{3,2,1,0:T(8,128)S(1)} %copy-done), kind=kLoop, calls=%fused_computation.6 | loop fusion | flops 2097152 | bytes 17825792 | tf_op jit(solution)/shard_map/stack | solution.py:144
  165.9 21.3 %collective-permute-done.2 = bf16[2,2,512,64]{3,2,1,0:T(8,128)(2,1)S(1)} collective-permute-done((bf16[2,2,512,64]{3,2,1,0:T(8,128)(2,1)S(1)}, bf16[2,2,512,64]{3,2,1,0:T(8,128)(2,1)S(1)}, u32[]{:S(2)}, u32[]{:S(2)}) %collective-permute-start.2) | collective-permute-done | bytes 262176 | tf_op jit(solution)/shard_map/ppermute | solution.py:63
  187.2 0.3 fusion.11
  187.6 5.8 %scatter-add.6 = f32[2,2,512,1024]{3,2,1,0:T(8,128)} dynamic-update-slice(f32[2,2,512,1024]{3,2,1,0:T(8,128)} %fusion.1, f32[2,2,512,64]{3,2,1,0:T(8,128)S(1)} %fusion.11, s32[]{:T(128)} %constant.217.clone.1, s32[]{:T(128)} %constant.217.clone.1, s32[]{:T(128)} %constant.217.clone.1, s32[]{:T(128)} %constant.217.clone.1) | dynamic-update-slice | bytes 1048580 | tf_op jit(solution)/shard_map/scatter-add | solution.py:150
  193.3 0.0 collective-permute-done.3
  193.3 1.6 slice_add_fusion
  194.9 5.8 %scatter-add.9 = f32[2,2,512,1024]{3,2,1,0:T(8,128)} dynamic-update-slice(f32[2,2,512,1024]{3,2,1,0:T(8,128)} %scatter-add.6, f32[2,2,512,64]{3,2,1,0:T(8,128)S(1)} %slice_add_fusion, s32[]{:T(128)} %constant.217.clone.1, s32[]{:T(128)} %constant.217.clone.1, s32[]{:T(128)} %constant.217.clone.1, s32[]{:T(128)} %constant.244.clone.1) | dynamic-update-slice | bytes 1048580 | tf_op jit(solution)/shard_map/scatter-add | solution.py:151
  200.7 6.1 %convert_bitcast_fusion = bf16[2,1,2,512,1024]{4,3,2,1,0:T(8,128)(2,1)} fusion(f32[2,2,512,1024]{3,2,1,0:T(8,128)} %scatter-add.9), kind=kLoop, calls=%fused_computation.7 | loop fusion | flops 2097152 | bytes 12582912 | tf_op jit(solution)/shard_map/broadcast_in_dim | solution.py:152
  (19 shorter events, 0.3 us)
Async XLA Ops:
  2.1 23.3 %collective-permute-start.1 = (bf16[2,2,512,64]{3,2,1,0:T(8,128)(2,1)S(1)}, bf16[2,2,512,64]{3,2,1,0:T(8,128)(2,1)S(1)}, u32[]{:S(2)}, u32[]{:S(2)}) collective-permute-start(bf16[2,2,512,64]{3,2,1,0:T(8,128)(2,1)S(1)} %get-tuple-element.30), channel_id=1, source_target_pairs={{1,0},{2,1},{3,2},{4,3},{5,4},{6,5},{7,6},{8,7},{9,8},{10,9},{11,1... | collective-permute-start | bytes 786440 | tf_op jit(solution)/shard_map/ppermute | solution.py:26
  9.8 22.8 %collective-permute-start = (bf16[2,2,512,64]{3,2,1,0:T(8,128)(2,1)S(1)}, bf16[2,2,512,64]{3,2,1,0:T(8,128)(2,1)S(1)}, u32[]{:S(2)}, u32[]{:S(2)}) collective-permute-start(bf16[2,2,512,64]{3,2,1,0:T(8,128)(2,1)S(1)} %get-tuple-element.31), channel_id=1, source_target_pairs={{0,1},{1,2},{2,3},{3,4},{4,5},{5,6},{6,7},{7,8},{8,9},{9,10},{10,1... | collective-permute-start | bytes 786440 | tf_op jit(solution)/shard_map/ppermute | solution.py:23
  45.5 21.4 %all-to-all-start.1 = ((bf16[16,2,32,1,128]{4,2,3,1,0:T(8,128)(2,1)}), bf16[16,2,32,1,128]{4,2,3,1,0:T(8,128)(2,1)S(1)}, u32[]{:S(2)}, u32[]{:S(2)}) async-start(bf16[16,2,32,1,128]{4,2,3,1,0:T(8,128)(2,1)} %maximum_bitcast_fusion.3), calls=%async_computation.1 | async-start | bytes 524288 | tf_op jit(solution)/shard_map/all_to_all | solution.py:38
  67.0 17.0 %all-to-all-start = ((bf16[16,2,32,1,128]{4,2,3,1,0:T(8,128)(2,1)}), bf16[16,2,32,1,128]{4,2,3,1,0:T(8,128)(2,1)S(1)}, u32[]{:S(2)}, u32[]{:S(2)}) async-start(bf16[16,2,32,1,128]{4,2,3,1,0:T(8,128)(2,1)} %maximum_bitcast_fusion.2), calls=%async_computation | async-start | bytes 524288 | tf_op jit(solution)/shard_map/all_to_all | solution.py:38
  97.0 19.8 %all-to-all-start.2 = ((f32[16,1,2,32,128]{4,3,2,1,0:T(8,128)}), f32[16,1,2,32,128]{4,3,2,1,0:T(8,128)S(1)}, u32[]{:S(2)}, u32[]{:S(2)}) async-start(f32[16,1,2,32,128]{4,3,2,1,0:T(8,128)} %broadcast_in_dim.11), calls=%async_computation.2 | async-start | bytes 1048576 | tf_op jit(solution)/shard_map/all_to_all | solution.py:44
  117.7 21.2 %all-to-all-start.3 = ((f32[16,1,2,32,128]{4,3,2,1,0:T(8,128)}), f32[16,1,2,32,128]{4,3,2,1,0:T(8,128)S(1)}, u32[]{:S(2)}, u32[]{:S(2)}) async-start(f32[16,1,2,32,128]{4,3,2,1,0:T(8,128)} %broadcast_in_dim.13), calls=%async_computation.3 | async-start | bytes 1048576 | tf_op jit(solution)/shard_map/all_to_all | solution.py:44
  147.5 13.3 %slice-start = ((s8[4718592]{0:T(1024)(128)(4,1)}), s8[524288]{0:T(1024)(128)(4,1)S(1)}, s32[]{:S(2)}) async-start(s8[4718592]{0:T(1024)(128)(4,1)} %bitcast.158), calls=%async_computation.4 | async-start | bytes 1048576
  151.4 9.4 %copy-start = (f32[1,2,512,1152]{3,2,1,0:T(8,128)S(1)}, f32[1,2,512,1152]{3,2,1,0:T(8,128)}, u32[]{:S(2)}) copy-start(f32[1,2,512,1152]{3,2,1,0:T(8,128)} %dynamic_update_slice.9) | copy-start | bytes 14155780
  151.4 9.4 %slice-start.1 = ((s8[4718592]{0:T(1024)(128)(4,1)}), s8[4194304]{0:T(1024)(128)(4,1)S(1)}, s32[]{:S(2)}) async-start(s8[4718592]{0:T(1024)(128)(4,1)} %bitcast.158), calls=%async_computation.5 | async-start | bytes 8388608
  156.3 37.1 %collective-permute-start.3 = (bf16[2,2,512,64]{3,2,1,0:T(8,128)(2,1)S(1)}, bf16[2,2,512,64]{3,2,1,0:T(8,128)(2,1)S(1)}, u32[]{:S(2)}, u32[]{:S(2)}) collective-permute-start(bf16[2,2,512,64]{3,2,1,0:T(8,128)(2,1)S(1)} %get-tuple-element.26), channel_id=1, source_target_pairs={{1,0},{2,1},{3,2},{4,3},{5,4},{6,5},{7,6},{8,7},{9,8},{10,9},{11,1... | collective-permute-start | bytes 786440 | tf_op jit(solution)/shard_map/ppermute | solution.py:63
  156.3 30.9 %collective-permute-start.2 = (bf16[2,2,512,64]{3,2,1,0:T(8,128)(2,1)S(1)}, bf16[2,2,512,64]{3,2,1,0:T(8,128)(2,1)S(1)}, u32[]{:S(2)}, u32[]{:S(2)}) collective-permute-start(bf16[2,2,512,64]{3,2,1,0:T(8,128)(2,1)S(1)} %get-tuple-element.27), channel_id=1, source_target_pairs={{15,0},{0,1},{1,2},{2,3},{3,4},{4,5},{5,6},{6,7},{7,8},{8,9},{9,10... | collective-permute-start | bytes 786440 | tf_op jit(solution)/shard_map/ppermute | solution.py:63
where the time goes:
time: 208 us; the launch traced here: 207 us
  waiting for transfers between devices  69.1 us (33%)
  local copies, waits for them, and re-layouts  43.4 us (21%)
  starting transfers between devices  42.3 us (20%)
  other arithmetic  22.8 us (11%)
  matrix products  19.1 us (9%)
  between operations  10.1 us (5%)
    all_to_all x2, waiting for transfers between devices, copy_for_each(): lax.all_to_all(jnp.broadcast_to(array[None], (devices, *array.shape)), ax...  21.7 us
    ppermute x2, waiting for transfers between devices, passed_along(): return lax.ppermute(block, axis, route)  21.3 us
    all_to_all x2, waiting for transfers between devices, sum_at_owner(): lax.all_to_all(split_up(array, dim, devices), axis, 0, 0, tiled=True)  18.9 us
    all_to_all x2, starting transfers between devices, sum_at_owner(): lax.all_to_all(split_up(array, dim, devices), axis, 0, 0, tiled=True)  16.2 us
    all_to_all x2, starting transfers between devices, copy_for_each(): lax.all_to_all(jnp.broadcast_to(array[None], (devices, *array.shape)), ax...  13.8 us
    concatenate x1, local copies, waits for them, and re-layouts, extended(): block = jnp.concatenate([low, block, high], axis=dim)  9.25 us
    ppermute x1, starting transfers between devices, extended(): lax.ppermute(lax.slice_in_dim(block, 0, width, axis=dim), axis, backward)  7.69 us
    dynamic_update_slice x2, local copies, waits for them, and re-layouts, per_device(): buffer = lax.dynamic_update_slice_in_dim(buffer, update, starts[0], 2)  7.38 us
  transfers between devices with their start and end apart: 8, of which 6 were waited for; matrix products, arithmetic and copies ran while one was open for 13% of the time, Pallas kernels for 0%

commit v1 on v0

v1 whole, which is shorter than its diff:
```python
import math

import jax
import jax.numpy as jnp
import numpy as np
from jax import lax
from jax.experimental import pallas as pl
from jax.experimental.pallas import tpu as pltpu
from jax.sharding import PartitionSpec as P

XM = 512
WM = 128
XA = 448
SHARD = 1024
HALF = WM // 2
FACETS = 16
F32 = jnp.float32
BF16 = jnp.bfloat16
I32 = jnp.int32
MESH = pl.DeviceIdType.MESH


def tables():
    place = np.arange(WM)
    cell = np.arange(XM)
    turns = (place[:, None] - WM // 2) * (cell[None, :] - XM // 2) % XM
    angle = 2.0 * math.pi * turns / XM
    relative = (place + 0.5 - WM / 2.0) / (WM / 2.0)
    taper = (0.3 + 0.7 * (1.0 - relative * relative)) / math.sqrt(WM * FACETS)
    real = (taper[:, None] * np.cos(angle)).astype(np.float32)
    imag = (taper[:, None] * np.sin(angle)).astype(np.float32)
    full = np.block([[real, imag], [-imag, real]])
    return full.astype(BF16), np.ascontiguousarray(full.T).astype(BF16)


def phase(turn):
    quarter = lax.shift_right_logical(turn + 8192, 14)
    angle = (turn - quarter * 16384).astype(F32) * (2.0 * math.pi / 65536.0)
    square = angle * angle
    sine = angle * (
        1.0 + square * (-1.0 / 6.0 + square * (1.0 / 120.0 + square * (-1.0 / 5040.0 + square * (1.0 / 362880.0))))
    )
    cosine = 1.0 + square * (-0.5 + square * (1.0 / 24.0 + square * (-1.0 / 720.0 + square * (1.0 / 40320.0))))
    odd = (quarter & 1) == 1
    first = jnp.where(odd, sine, cosine)
    second = jnp.where(odd, cosine, sine)
    cosine = jnp.where(((quarter + 1) & 2) == 2, -first, first)
    sine = jnp.where((quarter & 2) == 2, -second, second)
    return cosine, sine


def turns(column_pos, first, second, k):
    return (column_pos * first + 4 * (k * second)) & 65535


def iota(shape, dim):
    return lax.broadcasted_iota(I32, shape, dim)


def dot(a, b):
    return jnp.dot(a, b, preferred_element_type=F32)


def exchange_kernel(
    offs_ref, colidx_ref, sub_ref, x_hbm, w_hbm, t_hbm, tt_hbm,
    grid_out, u_out,
    x_v, w_v, t_v, tt_v, y, r1, r2a, r2b, rl, rr, s2, r3, above, below, eo, g,
    grid_v, local_sem, ss, rs,
):
    f = lax.axis_index("facet")
    c = lax.axis_index("col")
    core = f % 2
    x = (f // 2) % 4
    zh = f // 8
    left = (x + 3) % 4
    right = (x + 1) % 4
    far = (x + 2) % 4
    f_core = f + 1 - 2 * core
    f_left = zh * 8 + left * 2 + core
    f_right = zh * 8 + right * 2 + core
    f_z = (f + 8) % 16
    c_prev = (c + 15) % 16
    c_next = (c + 1) % 16

    barrier = pltpu.get_barrier_semaphore()
    peers = [
        (f_core, c), (f_left, c), (f_right, c), (f_z, c),
        (f, c_prev), (f_z, c_prev), (f, c_next), (f_z, c_next),
    ]
    for peer in peers:
        pl.semaphore_signal(barrier, inc=1, device_id=peer, device_id_type=MESH)

    loads = [
        pltpu.make_async_copy(x_hbm.at[0], x_v.at[0], local_sem.at[0]),
        pltpu.make_async_copy(x_hbm.at[1], x_v.at[1], local_sem.at[1]),
        pltpu.make_async_copy(t_hbm, t_v, local_sem.at[2]),
        pltpu.make_async_copy(tt_hbm, tt_v, local_sem.at[3]),
        pltpu.make_async_copy(w_hbm, w_v, local_sem.at[4]),
    ]
    for load in loads:
        load.start()

    sends = []

    def send(src, dst, f_to, c_to=None):
        index = len(sends)
        copy = pltpu.make_async_remote_copy(
            src_ref=src, dst_ref=dst, send_sem=ss.at[index], recv_sem=rs.at[index],
            device_id=(f_to, c if c_to is None else c_to), device_id_type=MESH,
        )
        copy.start()
        sends.append(copy)
        return copy

    lane = iota((16, 128), 1)
    starts = []

    def phased(col):
        position = lax.shift_right_arithmetic(sub_ref[col, 0], 2)
        start = position - c * SHARD - HALF
        starts.append(start)
        column_pos = colidx_ref[col] * XA
        first, second = offs_ref[0, 0], offs_ref[0, 1]
        cosine, sine = phase(turns(column_pos, first, second, c * SHARD + start + iota((8, 128), 1)))
        cosine, sine = cosine[0:1], sine[0:1]
        spot = iota((8, 128), 1)
        spot = c * SHARD + jnp.where(spot < HALF, spot, SHARD - 128 + spot)
        cosine_e, sine_e = phase(turns(column_pos, first, second, spot))
        cosine_e, sine_e = cosine_e[0:1], sine_e[0:1]
        pick = (iota((SHARD, 128), 0) == iota((SHARD, 128), 1) + start).astype(F32).astype(BF16)
        wide = iota((128, 128), 1) < HALF

        def rows(q, carry):
            span = pl.ds(pl.multiple_of(q * 128, 128), 128)
            main_re = dot(x_v[col, 0, span], pick)
            main_im = dot(x_v[col, 1, span], pick)
            out_re = (main_re * cosine + main_im * sine).astype(BF16)
            out_im = (main_im * cosine - main_re * sine).astype(BF16)
            edge_re = jnp.where(wide, x_v[col, 0, span, 0:128].astype(F32), x_v[col, 0, span, SHARD - 128:SHARD].astype(F32))
            edge_im = jnp.where(wide, x_v[col, 1, span, 0:128].astype(F32), x_v[col, 1, span, SHARD - 128:SHARD].astype(F32))
            e_re = edge_re * cosine_e + edge_im * sine_e
            e_im = edge_im * cosine_e - edge_re * sine_e
            swap_re = pltpu.roll(e_re, 64, 1)
            swap_im = pltpu.roll(e_im, 64, 1)
            for j in range(4):
                xx, cc = (q % 2) * 2 + j // 2, j % 2
                block = y.at[col, cc, xx, q // 2]
                a, b, d = 32 * j, 32 * j + 16, 32 * j + 32
                block[0:32] = out_re[a:d]
                block[32:64] = out_im[a:d]
                block[64:80] = jnp.where(lane < HALF, e_re[a:b], swap_re[b:d]).astype(BF16)
                block[80:96] = jnp.where(lane < HALF, e_im[a:b], swap_im[b:d]).astype(BF16)
                block[96:112] = jnp.where(lane < HALF, swap_re[a:b], e_re[b:d]).astype(BF16)
                block[112:128] = jnp.where(lane < HALF, swap_im[a:b], e_im[b:d]).astype(BF16)
            return carry

        lax.fori_loop(0, 4, rows, 0)

    order = [far, right, left, x]
    stage1 = []
    for col in range(2):
        loads[col].wait()
        phased(col)
        if col == 0:
            pl.semaphore_wait(barrier, len(peers))
        stage1.append([send(y.at[col, 1 - core, xx], r1.at[col, xx], f_core) for xx in order])

    def add(dst, *others):
        total = dst[...].astype(F32)
        for other in others:
            total = total + other[...].astype(F32)
        return total

    far_sent, near_sent = [], []
    for col in range(2):
        mine = y.at[col, core]
        stage1[col][0].wait_recv()
        mine[far] = add(mine.at[far], r1.at[col, far]).astype(BF16)
        far_sent.append((
            send(mine.at[far, 0], r2a.at[col], f_right),
            send(mine.at[far, 1], r2b.at[col], f_left),
        ))
        stage1[col][1].wait_recv()
        mine[right] = add(mine.at[right], r1.at[col, right]).astype(BF16)
        stage1[col][2].wait_recv()
        to_right = send(mine.at[right, 1], rl.at[col, 1], f_right)
        mine[left] = add(mine.at[left], r1.at[col, left]).astype(BF16)
        to_left = send(mine.at[left, 0], rr.at[col, 0], f_left)
        near_sent.append([to_right, to_left])

    for col in range(2):
        mine = y.at[col, core]
        far_sent[col][0].wait_recv()
        mine[right, 0] = add(mine.at[right, 0], r2a.at[col]).astype(BF16)
        near_sent[col].append(send(mine.at[right, 0], rl.at[col, 0], f_right))
        far_sent[col][1].wait_recv()
        mine[left, 1] = add(mine.at[left, 1], r2b.at[col]).astype(BF16)
        near_sent[col].append(send(mine.at[left, 1], rr.at[col, 1], f_left))
        stage1[col][3].wait_recv()

    stage3 = []
    other = 1 - zh
    for col in range(2):
        for copy in near_sent[col]:
            copy.wait_recv()
        mine = y.at[col, core, x]
        for zz in (other, zh):
            s2[col, zz] = add(mine.at[zz], r1.at[col, x, zz], rl.at[col, zz], rr.at[col, zz]).astype(BF16)
        copies = [send(s2.at[col, other, pl.ds(0, 64)], r3.at[col], f_z)]
        for k, (zz, f_to) in enumerate(((zh, f), (other, f_z))):
            copies.append(send(s2.at[col, zz, pl.ds(64, 32)], above.at[col, k], f_to, c_prev))
            copies.append(send(s2.at[col, zz, pl.ds(96, 32)], below.at[col, k], f_to, c_next))
        stage3.append(copies)

    for load in loads[2:]:
        load.wait()

    stage5 = []
    for col in range(2):
        start = starts[col]
        side0, side1 = iota((256, 256), 0), iota((256, 256), 1)

        def matrix(source, window):
            cell = (source & 63) + jnp.where(source < 128, -HALF, SHARD) - start
            same = (lax.shift_right_logical(source, 6) & 1) == lax.shift_right_logical(window, 7)
            return jnp.where(same & (cell == (window & 127)), 1.0, 0.0).astype(BF16)

        gather_in = matrix(side0, side1)
        gather_out = matrix(side1, side0)
        for copy in stage3[col]:
            copy.wait_recv()
        main = add(s2.at[col, zh, pl.ds(0, 64)], r3.at[col])
        low = add(below.at[col, 0], below.at[col, 1])
        high = add(above.at[col, 0], above.at[col, 1])
        edge = dot(jnp.concatenate([low, high], axis=1).astype(BF16), gather_in)
        edge_re = jnp.concatenate([edge[0:16, 0:128], edge[0:16, 128:256]], axis=0)
        edge_im = jnp.concatenate([edge[16:32, 0:128], edge[16:32, 128:256]], axis=0)
        window = jnp.concatenate([main[0:32] + edge_re, main[32:64] + edge_im], axis=1).astype(BF16)
        cells = dot(window, t_v[...]).astype(BF16)
        grid_v[col, 0] = cells[:, 0:XM]
        grid_v[col, 1] = cells[:, XM:2 * XM]
        weight = w_v[col].astype(F32)
        weight = jnp.concatenate([weight, weight], axis=1)
        scaled = (cells.astype(F32) * weight).astype(BF16)
        back = dot(scaled, tt_v[...]).astype(BF16)
        block = g.at[col, zh, x, core]
        block[0:32] = back[:, 0:128]
        block[32:64] = back[:, 128:256]
        packed = jnp.concatenate([
            jnp.concatenate([back[0:16, 0:128], back[16:32, 0:128]], axis=1),
            jnp.concatenate([back[0:16, 128:256], back[16:32, 128:256]], axis=1),
        ], axis=0)
        out_edge = dot(packed, gather_out).astype(BF16)
        eo[col, 0] = out_edge[:, 0:128]
        eo[col, 1] = out_edge[:, 128:256]
        home = g.at[col, zh, x, core]
        copies = [send(home.at[pl.ds(0, 64)], home.at[pl.ds(0, 64)], f_z)]
        for f_to in (f, f_z):
            copies.append(send(eo.at[col, 0], home.at[pl.ds(96, 32)], f_to, c_prev))
            copies.append(send(eo.at[col, 1], home.at[pl.ds(64, 32)], f_to, c_next))
        stage5.append(copies)

    grid_copy = pltpu.make_async_copy(grid_v, grid_out, local_sem.at[5])
    grid_copy.start()

    stage6 = []
    for col in range(2):
        for copy in stage5[col]:
            copy.wait_recv()
        block = g.at[col, :, x, core]
        stage6.append([send(block, block, f_right), send(block, block, f_left), send(block, block, f_core)])

    stage7, to_core = [], []
    for col in range(2):
        stage6[col][0].wait_recv()
        block = g.at[col, 0, left, core]
        onward = [send(block, block, f_right)]
        block = g.at[col, :, left, core]
        to_core.append([stage6[col][2], send(block, block, f_core)])
        stage6[col][1].wait_recv()
        block = g.at[col, 1, right, core]
        onward.append(send(block, block, f_left))
        block = g.at[col, :, right, core]
        to_core[col].append(send(block, block, f_core))
        stage7.append(onward)

    outs = []
    for col in range(2):
        for copy in stage7[col]:
            copy.wait_recv()
        block = g.at[col, :, far, core]
        to_core[col].append(send(block, block, f_core))
        for copy in to_core[col]:
            copy.wait_recv()
        out = pltpu.make_async_copy(g.at[col], u_out.at[col], local_sem.at[6 + col])
        out.start()
        outs.append(out)

    for copy in sends:
        copy.wait_send()
    grid_copy.wait()
    for out in outs:
        out.wait()


N_SENDS = 8 + 4 + 4 + 4 + 10 + 10 + 6 + 8 + 2


def exchange(offsets, column_index, subgrid_offsets, spectra, weights):
    table, table_t = tables()
    any_space = pl.BlockSpec(memory_space=pl.ANY)
    hbm = pl.BlockSpec(memory_space=pltpu.HBM)
    smem = pl.BlockSpec(memory_space=pltpu.SMEM)
    return pl.pallas_call(
        exchange_kernel,
        out_shape=(
            jax.ShapeDtypeStruct((2, 2, 32, XM), BF16),
            jax.ShapeDtypeStruct((2, 2, 4, 2, 128, 128), BF16),
        ),
        in_specs=[smem, smem, smem, hbm, hbm, hbm, hbm],
        out_specs=(any_space, any_space),
        scratch_shapes=[
            pltpu.VMEM((2, 2, XM, SHARD), BF16),
            pltpu.VMEM((2, 32, XM), BF16),
            pltpu.VMEM((256, 1024), BF16),
            pltpu.VMEM((1024, 256), BF16),
            pltpu.VMEM((2, 2, 4, 2, 128, 128), BF16),
            pltpu.VMEM((2, 4, 2, 128, 128), BF16),
            pltpu.VMEM((2, 128, 128), BF16),
            pltpu.VMEM((2, 128, 128), BF16),
            pltpu.VMEM((2, 2, 128, 128), BF16),
            pltpu.VMEM((2, 2, 128, 128), BF16),
            pltpu.VMEM((2, 2, 128, 128), BF16),
            pltpu.VMEM((2, 64, 128), BF16),
            pltpu.VMEM((2, 2, 32, 128), BF16),
            pltpu.VMEM((2, 2, 32, 128), BF16),
            pltpu.VMEM((2, 2, 32, 128), BF16),
            pltpu.VMEM((2, 2, 4, 2, 128, 128), BF16),
            pltpu.VMEM((2, 2, 32, XM), BF16),
            pltpu.SemaphoreType.DMA((8,)),
            pltpu.SemaphoreType.DMA((N_SENDS,)),
            pltpu.SemaphoreType.DMA((N_SENDS,)),
        ],
        compiler_params=pltpu.CompilerParams(
            collective_id=0, has_side_effects=True, vmem_limit_bytes=40 << 20
        ),
        name="exchange",
    )(offsets, column_index, subgrid_offsets, spectra, weights, jnp.asarray(table), jnp.asarray(table_t))


def place_kernel(offs_ref, colidx_ref, sub_ref, here_ref, u_ref, grid_ref, out_ref, grid_out):
    col = pl.program_id(0)
    c = here_ref[0]
    grid_out[...] = grid_ref[...]
    out_ref[...] = jnp.zeros_like(out_ref)
    position = lax.shift_right_arithmetic(sub_ref[col, 0], 2)
    start = position - c * SHARD - HALF
    base = jnp.clip(lax.shift_right_arithmetic(start, 7), 0, SHARD // 128 - 2) * 128
    column_pos = colidx_ref[col] * XA
    first, second = offs_ref[0, 0], offs_ref[0, 1]
    cosine, sine = phase(turns(column_pos, first, second, c * SHARD + base + iota((8, 256), 1)))
    cosine, sine = cosine[0:1], sine[0:1]
    spot = iota((8, 128), 1)
    spot = c * SHARD + jnp.where(spot < HALF, spot, SHARD - 128 + spot)
    cosine_e, sine_e = phase(turns(column_pos, first, second, spot))
    cosine_e, sine_e = cosine_e[0:1], sine_e[0:1]
    put = (iota((128, 256), 1) + base == iota((128, 256), 0) + start).astype(F32).astype(BF16)
    lane = iota((16, 128), 1)
    wide = iota((32, 128), 1) < HALF
    blocks = u_ref.shape[2]
    tiles = pl.ds(pl.multiple_of(base, 128), 256)
    for xx in range(blocks):
        for cc in range(2):
            block = u_ref.at[0, 0, xx, cc]
            rows = pl.ds((xx * 2 + cc) * 32, 32)
            low_re, low_im = block[64:80].astype(F32), block[80:96].astype(F32)
            top_re, top_im = block[96:112].astype(F32), block[112:128].astype(F32)
            edges = []
            for low, top in ((low_re, top_re), (low_im, top_im)):
                edges.append(jnp.concatenate([
                    jnp.where(lane < HALF, low, pltpu.roll(top, 64, 1)),
                    jnp.where(lane < HALF, pltpu.roll(low, 64, 1), top),
                ], axis=0))
            edge_re = edges[0] * cosine_e - edges[1] * sine_e
            edge_im = edges[1] * cosine_e + edges[0] * sine_e
            zero = jnp.zeros_like(edge_re)
            for part, edge in ((0, edge_re), (1, edge_im)):
                out_ref[0, part, rows, 0:128] = jnp.where(wide, edge, zero).astype(BF16)
                out_ref[0, part, rows, SHARD - 128:SHARD] = jnp.where(wide, zero, edge).astype(BF16)
            moved = dot(block[0:64], put)
            main_re, main_im = moved[0:32], moved[32:64]
            out_re = main_re * cosine - main_im * sine
            out_im = main_im * cosine + main_re * sine
            for part, value in ((0, out_re), (1, out_im)):
                out_ref[0, part, rows, tiles] = (out_ref[0, part, rows, tiles].astype(F32) + value).astype(BF16)


def place(offsets, column_index, subgrid_offsets, here, gathered, grids):
    smem = pl.BlockSpec(memory_space=pltpu.SMEM)
    return pl.pallas_call(
        place_kernel,
        grid=(2, 2),
        out_shape=(
            jax.ShapeDtypeStruct((2, 2, XM, SHARD), BF16),
            jax.ShapeDtypeStruct((2, 2, 32, XM), BF16),
        ),
        in_specs=[
            smem, smem, smem, smem,
            pl.BlockSpec((1, 1, 4, 2, 128, 128), lambda i, j: (i, j, 0, 0, 0, 0)),
            pl.BlockSpec((1, 2, 32, XM), lambda i, j: (i, 0, 0, 0)),
        ],
        out_specs=(
            pl.BlockSpec((1, 2, XM // 2, SHARD), lambda i, j: (i, 0, j, 0)),
            pl.BlockSpec((1, 2, 32, XM), lambda i, j: (i, 0, 0, 0)),
        ),
        compiler_params=pltpu.CompilerParams(dimension_semantics=("arbitrary", "arbitrary")),
        name="place",
    )(offsets, column_index, subgrid_offsets, here, gathered, grids)


def per_device(facet_spectra, facet_offsets, column_index, subgrid_offsets, weights):
    spectra = facet_spectra.reshape(2, 2, XM, SHARD)
    grids, gathered = exchange(
        facet_offsets, column_index, subgrid_offsets, spectra, weights.reshape(2, 32, XM)
    )
    here = lax.axis_index("col").astype(I32).reshape(1)
    updates, grids = place(facet_offsets, column_index, subgrid_offsets, here, gathered, grids)
    return grids.reshape(2, 1, 2, 32, XM), updates.reshape(2, 1, 2, XM, SHARD)


def solution(mesh):
    in_specs = (
        P(None, "facet", None, None, "col"),
        P("facet", None),
        P(),
        P(None, "col"),
        P(None, "col", "facet", None),
    )
    out_specs = (P(None, "col", None, "facet", None), P(None, "facet", None, None, "col"))
    return jax.shard_map(
        per_device, mesh=mesh, in_specs=in_specs, out_specs=out_specs, check_vma=False
    )
```

time: 208 us -> 53.9 us (0.26)
  waiting for transfers between devices: 69.1 us -> 0 us
  Pallas kernels: 0 us -> 44 us
  starting transfers between devices: 42.3 us -> 0 us
  local copies, waits for them, and re-layouts: 43.4 us -> 8.79 us
  other arithmetic: 22.8 us -> 0 us
  matrix products: 19.1 us -> 0 us
  between operations: 10.1 us -> 0.66 us
    pallas_call x0 -> x2, Pallas kernels: none -> 44 us  [the longest x1 39.4 us: exchange(): pl.pallas_call(exchange_kernel, out_shape=(jax.ShapeDtypeStruct((2, 2, 32...]
    all_to_all x4 -> x0, waiting for transfers between devices: 40.6 us -> none  [the longest x2 21.7 us: copy_for_each(): lax.all_to_all(jnp.broadcast_to(array[None], (devices, *array.shape)), ax...]
    all_to_all x4 -> x0, starting transfers between devices: 30.1 us -> none  [the longest x2 16.2 us: sum_at_owner(): lax.all_to_all(split_up(array, dim, devices), axis, 0, 0, tiled=True)]
    ppermute x4 -> x0, waiting for transfers between devices: 28.5 us -> none  [the longest x2 21.3 us: passed_along(): return lax.ppermute(block, axis, route)]
    dot_general x16 -> x0, matrix products: 19.1 us -> none  [the longest x2 2.54 us: per_device(): jnp.einsum('sxl,ml->sxm', scaled[:, 0], imag_tab, preferred_element_type=...]
    ppermute x4 -> x0, starting transfers between devices: 12.2 us -> none  [the longest x1 7.69 us: extended(): lax.ppermute(lax.slice_in_dim(block, 0, width, axis=dim), axis, backward)]
    scatter-add x2 -> x0, local copies, waits for them, and re-layouts: 11.6 us -> none  [the longest x1 5.82 us: per_device(): middle = middle.at[..., shard - half:].add(from_above)]
    another operation x5 -> x0, other arithmetic: 10.5 us -> none  [the longest x3 5.21 us: per_device(): stacked = jnp.stack(buffers)]
  transfers between devices with their start and end apart: 8 -> 0, of which waited for: 6 -> 0; matrix products, arithmetic and copies ran while one was open for 13% -> 0% of each run, Pallas kernels for 0% -> 0%
where the time goes in v1:
time: 53.9 us; the launch traced here: 53.5 us
  Pallas kernels  44 us (82%)
  local copies, waits for them, and re-layouts  8.79 us (16%)
  between operations  0.66 us (1%)
    pallas_call x1, Pallas kernels, exchange(): pl.pallas_call(exchange_kernel, out_shape=(jax.ShapeDtypeStruct((2, 2, 32...  39.4 us
    unnamed x19, local copies, waits for them, and re-layouts  8.79 us
    pallas_call x1, Pallas kernels, place(): pl.pallas_call(place_kernel, grid=(2, 2), out_shape=(jax.ShapeDtypeStruct...  4.61 us

profile of v1, /device:TPU:1, one launch (start us, length us, event | category | flops | bytes accessed | tf_op | source)
XLA Modules:
  0.0 53.5 jit_solution(4843407608694802198)
XLA Ops:
  0.6 0.7 %copy.10.sub_ref = s32[2,1]{1,0:T(2,128)S(1)} copy(s32[2,1]{0,1:T(1,128)} %param.10) | data formatting | bytes 16 | tf_op args[3]
  1.4 0.0 copy-start
  1.4 2.2 %copy-done = bf16[2,1,2,512,1024]{4,3,2,1,0:T(8,128)(2,1)S(1)} copy-done((bf16[2,1,2,512,1024]{4,3,2,1,0:T(8,128)(2,1)S(1)}, bf16[2,1,2,512,1024]{4,3,2,1,0:T(8,128)(2,1)}, u32[]{:S(2)}) %copy-start) | copy-done | bytes 4194328
  3.6 0.0 copy-start.2
  3.6 1.0 %copy-done.2 = bf16[1024,256]{1,0:T(8,128)(2,1)S(1)} copy-done((bf16[1024,256]{1,0:T(8,128)(2,1)S(1)}, bf16[1024,256]{1,0:T(8,128)(2,1)}, u32[]{:S(2)}) %copy-start.2) | copy-done | bytes 524312
  4.6 0.0 copy-start.3
  4.6 1.0 %copy-done.3 = bf16[256,1024]{1,0:T(8,128)(2,1)S(1)} copy-done((bf16[256,1024]{1,0:T(8,128)(2,1)S(1)}, bf16[256,1024]{1,0:T(8,128)(2,1)}, u32[]{:S(2)}) %copy-start.3) | copy-done | bytes 524312
  5.6 0.0 copy-start.5
  5.7 0.8 %copy-done.5 = bf16[2,1,32,512]{3,2,1,0:T(8,128)(2,1)S(1)} copy-done((bf16[2,1,32,512]{3,2,1,0:T(8,128)(2,1)S(1)}, bf16[2,1,32,512]{3,2,1,0:T(8,128)(2,1)}, u32[]{:S(2)}) %copy-start.5) | copy-done | bytes 65560
  6.5 0.0 copy-start.7
  6.5 0.7 %copy-done.7 = s32[1,2]{1,0:T(1,128)S(1)} copy-done((s32[1,2]{1,0:T(1,128)S(1)}, s32[1,2]{1,0:T(1,128)}, u32[]{:S(2)}) %copy-start.7) | copy-done | bytes 32
  7.1 0.0 copy-start.8
  7.1 0.7 %copy-done.8 = s32[2]{0:T(128)S(1)} copy-done((s32[2]{0:T(128)S(1)}, s32[2]{0:T(128)}, u32[]{:S(2)}) %copy-start.8) | copy-done | bytes 32
  7.8 0.0 copy-start.6
  7.8 39.4 %exchange.1 = (bf16[2,2,32,512]{3,2,1,0:T(8,128)(2,1)S(1)}, bf16[2,2,4,2,128,128]{5,4,3,2,1,0:T(8,128)(2,1)S(1)}) custom-call(s32[1,2]{1,0:T(1,128)S(1)} %copy-done.7, s32[2]{0:T(128)S(1)} %copy-done.8, s32[2,1]{1,0:T(2,128)S(1)} %copy.10.sub_ref, bf16[2,2,512,1024]{3,2,1,0:T(8,128)(2,1)S(1)} %bitcast.9, bf16[2,32,512]{2,1,0:T(8,128)(2,1)S(1)} %bitcast.10, ...), custom_call_target="tpu_custom_call" | custom-call | tf_op jit(solution)/shard_map/exchange/pallas_call | solution.py:314
  47.2 0.0 copy-start.1
  47.2 1.0 %copy-done.1 = bf16[2,2,4,2,128,128]{5,4,3,2,1,0:T(8,128)(2,1)} copy-done((bf16[2,2,4,2,128,128]{5,4,3,2,1,0:T(8,128)(2,1)}, bf16[2,2,4,2,128,128]{5,4,3,2,1,0:T(8,128)(2,1)S(1)}, u32[]{:S(2)}) %copy-start.1) | copy-done | bytes 1048600
  48.2 0.0 copy-start.4
  48.2 0.7 %copy-done.4 = bf16[2,2,32,512]{3,2,1,0:T(8,128)(2,1)} copy-done((bf16[2,2,32,512]{3,2,1,0:T(8,128)(2,1)}, bf16[2,2,32,512]{3,2,1,0:T(8,128)(2,1)S(1)}, u32[]{:S(2)}) %copy-start.4) | copy-done | bytes 131096
  48.8 0.0 copy-done.6
  48.8 4.6 %place.1 = (bf16[2,2,512,1024]{3,2,1,0:T(8,128)(2,1)}, bf16[2,2,32,512]{3,2,1,0:T(8,128)(2,1)}) custom-call(s32[1,2]{1,0:T(1,128)} %offs_ref.3, s32[2]{0:T(128)} %colidx_ref.3, s32[2,1]{1,0:T(2,128)} %copy-done.6, s32[1]{0:T(128)} %bitcast.here_ref, bf16[2,2,4,2,128,128]{5,4,3,2,1,0:T(8,128)(2,1)} %copy-done.1, bf16[2,2,32,512]{3,2,1,0:T(8,128)(2,1)} %copy-done.4), custom_call_target="tpu_custom_call" | custom-call | tf_op jit(solution)/shard_map/place/pallas_call | solution.py:400
Async XLA Ops:
  1.4 2.2 %copy-start = (bf16[2,1,2,512,1024]{4,3,2,1,0:T(8,128)(2,1)S(1)}, bf16[2,1,2,512,1024]{4,3,2,1,0:T(8,128)(2,1)}, u32[]{:S(2)}) copy-start(bf16[2,1,2,512,1024]{4,3,2,1,0:T(8,128)(2,1)} %param.7) | copy-start | bytes 12582916
  3.6 1.0 %copy-start.2 = (bf16[1024,256]{1,0:T(8,128)(2,1)S(1)}, bf16[1024,256]{1,0:T(8,128)(2,1)}, u32[]{:S(2)}) copy-start(bf16[1024,256]{1,0:T(8,128)(2,1)} %constant.9.clone.tt_hbm) | copy-start | bytes 1572868
  4.6 1.0 %copy-start.3 = (bf16[256,1024]{1,0:T(8,128)(2,1)S(1)}, bf16[256,1024]{1,0:T(8,128)(2,1)}, u32[]{:S(2)}) copy-start(bf16[256,1024]{1,0:T(8,128)(2,1)} %constant.8.clone.t_hbm) | copy-start | bytes 1572868
  5.6 0.8 %copy-start.5 = (bf16[2,1,32,512]{3,2,1,0:T(8,128)(2,1)S(1)}, bf16[2,1,32,512]{3,2,1,0:T(8,128)(2,1)}, u32[]{:S(2)}) copy-start(bf16[2,1,32,512]{3,2,1,0:T(8,128)(2,1)} %param.11) | copy-start | bytes 196612
  6.5 0.7 %copy-start.7 = (s32[1,2]{1,0:T(1,128)S(1)}, s32[1,2]{1,0:T(1,128)}, u32[]{:S(2)}) copy-start(s32[1,2]{1,0:T(1,128)} %offs_ref.3) | copy-start | bytes 28
  7.1 0.7 %copy-start.8 = (s32[2]{0:T(128)S(1)}, s32[2]{0:T(128)}, u32[]{:S(2)}) copy-start(s32[2]{0:T(128)} %colidx_ref.3) | copy-start | bytes 28
  7.8 41.0 %copy-start.6 = (s32[2,1]{1,0:T(2,128)}, s32[2,1]{1,0:T(2,128)S(1)}, u32[]{:S(2)}) copy-start(s32[2,1]{1,0:T(2,128)S(1)} %copy.10.sub_ref) | copy-start | bytes 28
  47.2 1.0 %copy-start.1 = (bf16[2,2,4,2,128,128]{5,4,3,2,1,0:T(8,128)(2,1)}, bf16[2,2,4,2,128,128]{5,4,3,2,1,0:T(8,128)(2,1)S(1)}, u32[]{:S(2)}) copy-start(bf16[2,2,4,2,128,128]{5,4,3,2,1,0:T(8,128)(2,1)S(1)} %get-tuple-element.6.u_ref) | copy-start | bytes 3145732
  48.2 0.7 %copy-start.4 = (bf16[2,2,32,512]{3,2,1,0:T(8,128)(2,1)}, bf16[2,2,32,512]{3,2,1,0:T(8,128)(2,1)S(1)}, u32[]{:S(2)}) copy-start(bf16[2,2,32,512]{3,2,1,0:T(8,128)(2,1)S(1)} %get-tuple-element.7.grid_ref) | copy-start | bytes 393220

commit v2 on v1

--- a/solution.py
+++ b/solution.py
@@ -116,7 +116,7 @@
     starts = []
 
     def phased(col):
-        position = lax.shift_right_arithmetic(sub_ref[col, 0], 2)
+        position = lax.shift_right_arithmetic(sub_ref[col], 2)
         start = position - c * SHARD - HALF
         starts.append(start)
         column_pos = colidx_ref[col] * XA
@@ -342,7 +342,7 @@
             pltpu.SemaphoreType.DMA((N_SENDS,)),
         ],
         compiler_params=pltpu.CompilerParams(
-            collective_id=0, has_side_effects=True, vmem_limit_bytes=40 << 20
+            collective_id=0, has_side_effects=True
         ),
         name="exchange",
     )(offsets, column_index, subgrid_offsets, spectra, weights, jnp.asarray(table), jnp.asarray(table_t))
@@ -353,7 +353,7 @@
     c = here_ref[0]
     grid_out[...] = grid_ref[...]
     out_ref[...] = jnp.zeros_like(out_ref)
-    position = lax.shift_right_arithmetic(sub_ref[col, 0], 2)
+    position = lax.shift_right_arithmetic(sub_ref[col], 2)
     start = position - c * SHARD - HALF
     base = jnp.clip(lax.shift_right_arithmetic(start, 7), 0, SHARD // 128 - 2) * 128
     column_pos = colidx_ref[col] * XA
@@ -420,6 +420,7 @@
 
 def per_device(facet_spectra, facet_offsets, column_index, subgrid_offsets, weights):
     spectra = facet_spectra.reshape(2, 2, XM, SHARD)
+    subgrid_offsets = subgrid_offsets.reshape(2)
     grids, gathered = exchange(
         facet_offsets, column_index, subgrid_offsets, spectra, weights.reshape(2, 32, XM)
     )

time: 53.9 us -> 46.1 us (0.86)
  local copies, waits for them, and re-layouts: 8.79 us -> 0 us
  Pallas kernels: 44 us -> 45.3 us
    unnamed x19 -> x0, local copies, waits for them, and re-layouts: 8.79 us -> none
    pallas_call x1, Pallas kernels: 39.4 us -> 40.7 us  [exchange(): pl.pallas_call(exchange_kernel, out_shape=(jax.ShapeDtypeStruct((2, 2, 32...]
where the time goes in v2:
time: 46.1 us; the launch traced here: 46 us
  Pallas kernels  45.3 us (98%)
  between operations  0.64 us (1%)
    pallas_call x1, Pallas kernels, exchange(): pl.pallas_call(exchange_kernel, out_shape=(jax.ShapeDtypeStruct((2, 2, 32...  40.7 us
    pallas_call x1, Pallas kernels, place(): pl.pallas_call(place_kernel, grid=(2, 2), out_shape=(jax.ShapeDtypeStruct...  4.64 us

profile of v2, /device:TPU:1, one launch (start us, length us, event | category | flops | bytes accessed | tf_op | source)
XLA Modules:
  0.0 46.0 jit_solution(8406042336679737917)
XLA Ops:
  0.6 40.7 %exchange.1 = (bf16[2,2,32,512]{3,2,1,0:T(8,128)(2,1)}, bf16[2,2,4,2,128,128]{5,4,3,2,1,0:T(8,128)(2,1)}) custom-call(s32[1,2]{1,0:T(1,128)} %offs_ref.3, s32[2]{0:T(128)} %colidx_ref.3, s32[2]{0:T(128)} %bitcast.12, bf16[2,2,512,1024]{3,2,1,0:T(8,128)(2,1)} %bitcast.10, bf16[2,32,512]{2,1,0:T(8,128)(2,1)} %bitcast.11, ...), custom_call_target="tpu_custom_call" | custom-call | tf_op jit(solution)/shard_map/exchange/pallas_call | solution.py:314
  41.3 4.6 %place.1 = (bf16[2,2,512,1024]{3,2,1,0:T(8,128)(2,1)}, bf16[2,2,32,512]{3,2,1,0:T(8,128)(2,1)}) custom-call(s32[1,2]{1,0:T(1,128)} %offs_ref.3, s32[2]{0:T(128)} %colidx_ref.3, s32[2]{0:T(128)} %bitcast.13, s32[1]{0:T(128)} %bitcast.1.here_ref, bf16[2,2,4,2,128,128]{5,4,3,2,1,0:T(8,128)(2,1)} %get-tuple-element.6.u_ref, ...), custom_call_target="tpu_custom_call" | custom-call | tf_op jit(solution)/shard_map/place/pallas_call | solution.py:400

commit v3 on v2

v3 whole, which is shorter than its diff:
```python
import math

import jax
import jax.numpy as jnp
import numpy as np
from jax import lax
from jax.experimental import pallas as pl
from jax.experimental.pallas import tpu as pltpu
from jax.sharding import PartitionSpec as P

XM = 512
WM = 128
XA = 448
SHARD = 1024
HALF = WM // 2
FACETS = 16
F32 = jnp.float32
BF16 = jnp.bfloat16
I32 = jnp.int32
MESH = pl.DeviceIdType.MESH


def tables():
    place = np.arange(WM)
    cell = np.arange(XM)
    turns = (place[:, None] - WM // 2) * (cell[None, :] - XM // 2) % XM
    angle = 2.0 * math.pi * turns / XM
    relative = (place + 0.5 - WM / 2.0) / (WM / 2.0)
    taper = (0.3 + 0.7 * (1.0 - relative * relative)) / math.sqrt(WM * FACETS)
    real = (taper[:, None] * np.cos(angle)).astype(np.float32)
    imag = (taper[:, None] * np.sin(angle)).astype(np.float32)
    wide = np.concatenate([real, imag], axis=1)
    tall = np.concatenate([real.T, imag.T], axis=1)
    return wide.astype(BF16), np.ascontiguousarray(tall).astype(BF16)


def phase(turn):
    quarter = lax.shift_right_logical(turn + 8192, 14)
    angle = (turn - quarter * 16384).astype(F32) * (2.0 * math.pi / 65536.0)
    square = angle * angle
    sine = angle * (
        1.0 + square * (-1.0 / 6.0 + square * (1.0 / 120.0 + square * (-1.0 / 5040.0 + square * (1.0 / 362880.0))))
    )
    cosine = 1.0 + square * (-0.5 + square * (1.0 / 24.0 + square * (-1.0 / 720.0 + square * (1.0 / 40320.0))))
    odd = (quarter & 1) == 1
    first = jnp.where(odd, sine, cosine)
    second = jnp.where(odd, cosine, sine)
    cosine = jnp.where(((quarter + 1) & 2) == 2, -first, first)
    sine = jnp.where((quarter & 2) == 2, -second, second)
    return cosine, sine


def turns(column_pos, first, second, k):
    return (column_pos * first + 4 * (k * second)) & 65535


def iota(shape, dim):
    return lax.broadcasted_iota(I32, shape, dim)


def dot(a, b):
    return jnp.dot(a, b, preferred_element_type=F32)


def exchange_kernel(
    offs_hbm, colidx_hbm, sub_hbm, x_hbm, w_hbm, t_hbm, tt_hbm,
    grid_out, g,
    offs_ref, colidx_ref, sub_ref, x_v, w_v, t_v, tt_v, y, r1, rx, s2, r3, above, below, eo,
    grid_v, local_sem, ss, rs,
):
    f = lax.axis_index("facet")
    c = lax.axis_index("col")
    core = f % 2
    x = (f // 2) % 4
    zh = f // 8
    z_lo = c % 4
    c_prev = (c + 15) % 16
    c_next = (c + 1) % 16
    zh_prev = jnp.where(z_lo == 0, 1 - zh, zh)
    zh_next = jnp.where(z_lo == 3, 1 - zh, zh)

    def facet(half, place_x, which):
        return half * 8 + place_x * 2 + which

    def x_of(d):
        return (x + d) % 4

    f_core = facet(zh, x, 1 - core)
    f_z = facet(1 - zh, x, core)
    f_x = [f] + [facet(zh, x_of(d), core) for d in (1, 2, 3)]

    barrier = pltpu.get_barrier_semaphore()
    peers = [(f_core, c), (f_z, c), (f_x[1], c), (f_x[2], c), (f_x[3], c)]
    peers += [(f, c_prev), (f_z, c_prev), (f, c_next), (f_z, c_next)]
    peers += [(facet(zh_prev, x_of(d), core), c_prev) for d in (1, 2, 3)]
    peers += [(facet(zh_next, x_of(d), core), c_next) for d in (1, 2, 3)]
    for peer in peers:
        pl.semaphore_signal(barrier, inc=1, device_id=peer, device_id_type=MESH)

    loads = [
        pltpu.make_async_copy(x_hbm.at[0], x_v.at[0], local_sem.at[0]),
        pltpu.make_async_copy(x_hbm.at[1], x_v.at[1], local_sem.at[1]),
        pltpu.make_async_copy(t_hbm, t_v, local_sem.at[2]),
        pltpu.make_async_copy(tt_hbm, tt_v, local_sem.at[3]),
        pltpu.make_async_copy(w_hbm, w_v.at[zh], local_sem.at[4]),
    ]
    scalars = [
        pltpu.make_async_copy(source, target, local_sem.at[6 + index])
        for index, (source, target) in enumerate(
            ((offs_hbm, offs_ref), (colidx_hbm, colidx_ref), (sub_hbm, sub_ref))
        )
    ]
    for load in scalars:
        load.start()
    loads[0].start()

    sends = []

    def send(src, dst, f_to, c_to=None):
        index = len(sends)
        copy = pltpu.make_async_remote_copy(
            src_ref=src, dst_ref=dst, send_sem=ss.at[index], recv_sem=rs.at[index],
            device_id=(f_to, c if c_to is None else c_to), device_id_type=MESH,
        )
        copy.start()
        sends.append(copy)
        return copy

    for load in scalars:
        load.wait()
    lane = iota((16, 128), 1)
    first, second = offs_ref[0, 0], offs_ref[0, 1]
    starts = []
    for col in range(2):
        starts.append(lax.shift_right_arithmetic(sub_ref[col], 2) - c * SHARD - HALF)

    def phased(col):
        start = starts[col]
        column_pos = colidx_ref[col] * XA
        cosine, sine = phase(turns(column_pos, first, second, c * SHARD + start + iota((8, 128), 1)))
        cosine, sine = cosine[0:1], sine[0:1]
        spot = iota((8, 128), 1)
        spot = c * SHARD + jnp.where(spot < HALF, spot, SHARD - 128 + spot)
        cosine_e, sine_e = phase(turns(column_pos, first, second, spot))
        cosine_e, sine_e = cosine_e[0:1], sine_e[0:1]
        tile = jnp.clip(lax.shift_right_arithmetic(start, 7), 0, SHARD // 128 - 2)
        pick = (iota((256, 128), 0) + tile * 128 == iota((256, 128), 1) + start).astype(F32).astype(BF16)
        bits = [(jnp.full((128, 128), 0, I32) + tile) & (1 << bit) != 0 for bit in range(3)]
        wide = iota((128, 128), 1) < HALF

        def rows(q, carry):
            span = pl.ds(pl.multiple_of(q * 128, 128), 128)
            pairs = []
            for part in range(2):
                tiles = [x_v[col, part, span, 128 * i:128 * i + 128] for i in range(8)]
                for bit, width in ((2, 5), (1, 3), (0, 2)):
                    far = 1 << bit
                    tiles = [
                        jnp.where(bits[bit], tiles[i + far], tiles[i]) if i + far < len(tiles) else tiles[i]
                        for i in range(width)
                    ]
                pairs.append(jnp.concatenate(tiles, axis=1))
            main_re = dot(pairs[0], pick)
            main_im = dot(pairs[1], pick)
            out_re = (main_re * cosine + main_im * sine).astype(BF16)
            out_im = (main_im * cosine - main_re * sine).astype(BF16)
            edge_re = jnp.where(wide, x_v[col, 0, span, 0:128].astype(F32), x_v[col, 0, span, SHARD - 128:SHARD].astype(F32))
            edge_im = jnp.where(wide, x_v[col, 1, span, 0:128].astype(F32), x_v[col, 1, span, SHARD - 128:SHARD].astype(F32))
            e_re = edge_re * cosine_e + edge_im * sine_e
            e_im = edge_im * cosine_e - edge_re * sine_e
            swap_re = pltpu.roll(e_re, 64, 1)
            swap_im = pltpu.roll(e_im, 64, 1)
            for j in range(4):
                xx, cc = (q % 2) * 2 + j // 2, j % 2
                block = y.at[col, cc, xx, q // 2]
                a, b, d = 32 * j, 32 * j + 16, 32 * j + 32
                block[0:32] = out_re[a:d]
                block[32:64] = out_im[a:d]
                block[64:80] = jnp.where(lane < HALF, e_re[a:b], swap_re[b:d]).astype(BF16)
                block[80:96] = jnp.where(lane < HALF, e_im[a:b], swap_im[b:d]).astype(BF16)
                block[96:112] = jnp.where(lane < HALF, swap_re[a:b], e_re[b:d]).astype(BF16)
                block[112:128] = jnp.where(lane < HALF, swap_im[a:b], e_im[b:d]).astype(BF16)
            return carry

        lax.fori_loop(0, 4, rows, 0)

    def total(*refs):
        result = refs[0][...].astype(F32)
        for ref in refs[1:]:
            result = result + ref[...].astype(F32)
        return result

    order = (2, 1, 3, 0)
    to_core = []
    weights_there = None
    for col in range(2):
        loads[col].wait()
        for load in loads[1:2] if col == 0 else loads[2:]:
            load.start()
        phased(col)
        if col == 0:
            pl.semaphore_wait(barrier, len(peers))
        to_core.append([send(y.at[col, 1 - core, x_of(d)], r1.at[col, x_of(d)], f_core) for d in order])
        if col == 0:
            weights_there = send(w_hbm, w_v.at[zh], f_z)

    to_x = []
    for col in range(2):
        copies = []
        for d, copy in zip(order, to_core[col]):
            copy.wait_recv()
            xx = x_of(d)
            if d:
                y[col, core, xx] = total(y.at[col, core, xx], r1.at[col, xx]).astype(BF16)
                copies.append(send(y.at[col, core, xx], rx.at[col, d - 1], f_x[d]))
        to_x.append(copies)

    to_z = []
    for col in range(2):
        for copy in to_x[col]:
            copy.wait_recv()
        s2[col] = total(
            y.at[col, core, x], r1.at[col, x], rx.at[col, 0], rx.at[col, 1], rx.at[col, 2]
        ).astype(BF16)
        copies = [send(s2.at[col, :, pl.ds(0, 64)], r3.at[col], f_z)]
        for k, f_to in enumerate((f, f_z)):
            copies.append(send(s2.at[col, :, pl.ds(64, 32)], above.at[col, k], f_to, c_prev))
            copies.append(send(s2.at[col, :, pl.ds(96, 32)], below.at[col, k], f_to, c_next))
        to_z.append(copies)

    for load in loads[2:]:
        load.wait()
    weights_there.wait_recv()

    to_all = []
    for col in range(2):
        start = starts[col]

        def matrix(source, window):
            cell = (source & 63) + jnp.where(source < 128, -HALF, SHARD) - start
            same = (lax.shift_right_logical(source, 6) & 1) == lax.shift_right_logical(window, 7)
            return jnp.where(same & (cell == (window & 127)), 1.0, 0.0).astype(BF16)

        side0, side1 = iota((256, 256), 0), iota((256, 256), 1)
        gather_in = matrix(side0, side1)
        gather_out = matrix(side1, side0)
        for copy in to_z[col]:
            copy.wait_recv()
        main = total(s2.at[col, :, pl.ds(0, 64)], r3.at[col])
        low = total(below.at[col, 0], below.at[col, 1]).reshape(64, 128)
        high = total(above.at[col, 0], above.at[col, 1]).reshape(64, 128)
        edge = dot(jnp.concatenate([low, high], axis=1).astype(BF16), gather_in)
        windows = []
        for part in range(2):
            for half in range(2):
                a = half * 32 + part * 16
                reach = jnp.concatenate([edge[a:a + 16, 0:128], edge[a:a + 16, 128:256]], axis=0)
                windows.append(main[half, part * 32:part * 32 + 32] + reach)
        window = jnp.concatenate(windows, axis=0).astype(BF16)
        prod = dot(window, t_v[...])
        cells_re = (prod[0:64, 0:XM] - prod[64:128, XM:2 * XM]).astype(BF16)
        cells_im = (prod[0:64, XM:2 * XM] + prod[64:128, 0:XM]).astype(BF16)
        weight = jnp.concatenate([w_v[0, col], w_v[1, col]], axis=0).astype(F32)
        scaled_re = (cells_re.astype(F32) * weight).astype(BF16)
        scaled_im = (cells_im.astype(F32) * weight).astype(BF16)
        prod = dot(jnp.concatenate([scaled_re, scaled_im], axis=0), tt_v[...])
        back_re = (prod[0:64, 0:WM] + prod[64:128, WM:2 * WM]).astype(BF16)
        back_im = (prod[64:128, 0:WM] - prod[0:64, WM:2 * WM]).astype(BF16)
        for half in range(2):
            grid_v[half, col, 0] = cells_re[half * 32:half * 32 + 32]
            grid_v[half, col, 1] = cells_im[half * 32:half * 32 + 32]
        packed = []
        for half in range(2):
            block = g.at[col, half, x, core]
            a = half * 32
            block[0:32] = back_re[a:a + 32]
            block[32:64] = back_im[a:a + 32]
            for back in (back_re, back_im):
                packed.append(jnp.concatenate([back[a:a + 16], back[a + 16:a + 32]], axis=1))
        out_edge = dot(jnp.concatenate(packed, axis=0), gather_out).astype(BF16)
        eo[col, 0] = out_edge[:, 0:128].reshape(2, 32, 128)
        eo[col, 1] = out_edge[:, 128:256].reshape(2, 32, 128)
        low, high = g.at[col, :, x, core, pl.ds(64, 32)], g.at[col, :, x, core, pl.ds(96, 32)]
        edges = []
        for d in order:
            edges.append((
                send(eo.at[col, 0], high, facet(zh_prev, x_of(d), core), c_prev),
                send(eo.at[col, 1], low, facet(zh_next, x_of(d), core), c_next),
            ))
        home = g.at[col, :, x, core, pl.ds(0, 64)]
        mains = [send(home, home, f_x[d]) for d in (2, 1, 3)]
        to_all.append((mains, edges, [send(home, home, f_core)]))

    grid_copy = pltpu.make_async_copy(grid_v.at[zh], grid_out, local_sem.at[5])
    grid_copy.start()

    for col in range(2):
        mains, edges, passed = to_all[col]
        for d, copy in ((1, mains[1]), (3, mains[2]), (2, mains[0])):
            copy.wait_recv()
            block = g.at[col, :, x_of(4 - d), core, pl.ds(0, 64)]
            passed.append(send(block, block, f_core))
        for d, pair in zip(order, edges):
            for copy in pair:
                copy.wait_recv()
            block = g.at[col, :, x_of(4 - d), core, pl.ds(64, 64)]
            passed.append(send(block, block, f_core))
    for col in range(2):
        for copy in to_all[col][2]:
            copy.wait_recv()

    for copy in sends:
        copy.wait_send()
    grid_copy.wait()


N_SENDS = 63


def exchange(offsets, column_index, subgrid_offsets, spectra, weights):
    table, table_t = tables()
    hbm = pl.BlockSpec(memory_space=pltpu.HBM)
    vmem = pl.BlockSpec(memory_space=pltpu.VMEM)
    return pl.pallas_call(
        exchange_kernel,
        out_shape=(
            pltpu.VMEM((2, 2, 32, XM), BF16),
            pltpu.VMEM((2, 2, 4, 2, 128, 128), BF16),
        ),
        in_specs=[hbm] * 7,
        out_specs=(vmem, vmem),
        scratch_shapes=[
            pltpu.SMEM((1, 2), I32),
            pltpu.SMEM((2,), I32),
            pltpu.SMEM((2,), I32),
            pltpu.VMEM((2, 2, XM, SHARD), BF16),
            pltpu.VMEM((2, 2, 32, XM), BF16),
            pltpu.VMEM((WM, 2 * XM), BF16),
            pltpu.VMEM((XM, 2 * WM), BF16),
            pltpu.VMEM((2, 2, 4, 2, 128, 128), BF16),
            pltpu.VMEM((2, 4, 2, 128, 128), BF16),
            pltpu.VMEM((2, 3, 2, 128, 128), BF16),
            pltpu.VMEM((2, 2, 128, 128), BF16),
            pltpu.VMEM((2, 2, 64, 128), BF16),
            pltpu.VMEM((2, 2, 2, 32, 128), BF16),
            pltpu.VMEM((2, 2, 2, 32, 128), BF16),
            pltpu.VMEM((2, 2, 2, 32, 128), BF16),
            pltpu.VMEM((2, 2, 2, 32, XM), BF16),
            pltpu.SemaphoreType.DMA((9,)),
            pltpu.SemaphoreType.DMA((N_SENDS,)),
            pltpu.SemaphoreType.DMA((N_SENDS,)),
        ],
        compiler_params=pltpu.CompilerParams(collective_id=0, has_side_effects=True),
        name="exchange",
    )(offsets, column_index, subgrid_offsets, spectra, weights, jnp.asarray(table), jnp.asarray(table_t))


def place_kernel(offs_ref, colidx_ref, sub_ref, here_ref, u_ref, grid_ref, out_hbm, grid_hbm, out, sem):
    grid_copy = pltpu.make_async_copy(grid_ref, grid_hbm, sem.at[0])
    grid_copy.start()
    c = here_ref[0]
    first, second = offs_ref[0, 0], offs_ref[0, 1]
    spot = iota((8, 128), 1)
    spot = c * SHARD + jnp.where(spot < HALF, spot, SHARD - 128 + spot)
    lane = iota((16, 128), 1)
    wide = iota((32, 128), 1) < HALF
    for col in range(2):
        start = lax.shift_right_arithmetic(sub_ref[col], 2) - c * SHARD - HALF
        base = jnp.clip(lax.shift_right_arithmetic(start, 7), 0, SHARD // 128 - 2) * 128
        column_pos = colidx_ref[col] * XA
        cosine, sine = phase(turns(column_pos, first, second, c * SHARD + base + iota((8, 256), 1)))
        cosine, sine = cosine[0:1], sine[0:1]
        cosine_e, sine_e = phase(turns(column_pos, first, second, spot))
        cosine_e, sine_e = cosine_e[0:1], sine_e[0:1]
        put = (iota((128, 256), 1) + base == iota((128, 256), 0) + start).astype(F32).astype(BF16)
        tiles = pl.ds(pl.multiple_of(base, 128), 256)

        def rows_of(q, carry):
            span = pl.ds(pl.multiple_of(q * 128, 128), 128)
            out[col, :, span] = jnp.zeros((2, 128, SHARD), BF16)
            for j in range(4):
                block = u_ref.at[col, q // 2, (q % 2) * 2 + j // 2, j % 2]
                rows = pl.ds(pl.multiple_of(q * 128 + 32 * j, 32), 32)
                low_re, low_im = block[64:80].astype(F32), block[80:96].astype(F32)
                top_re, top_im = block[96:112].astype(F32), block[112:128].astype(F32)
                edges = []
                for low, top in ((low_re, top_re), (low_im, top_im)):
                    edges.append(jnp.concatenate([
                        jnp.where(lane < HALF, low, pltpu.roll(top, 64, 1)),
                        jnp.where(lane < HALF, pltpu.roll(low, 64, 1), top),
                    ], axis=0))
                edge_re = edges[0] * cosine_e - edges[1] * sine_e
                edge_im = edges[1] * cosine_e + edges[0] * sine_e
                zero = jnp.zeros_like(edge_re)
                for part, edge in ((0, edge_re), (1, edge_im)):
                    out[col, part, rows, 0:128] = jnp.where(wide, edge, zero).astype(BF16)
                    out[col, part, rows, SHARD - 128:SHARD] = jnp.where(wide, zero, edge).astype(BF16)
                moved = dot(block[0:64], put)
                main_re, main_im = moved[0:32], moved[32:64]
                out_re = main_re * cosine - main_im * sine
                out_im = main_im * cosine + main_re * sine
                for part, value in ((0, out_re), (1, out_im)):
                    out[col, part, rows, tiles] = (out[col, part, rows, tiles].astype(F32) + value).astype(BF16)
            pltpu.make_async_copy(out.at[col, :, span], out_hbm.at[col, :, span], sem.at[1 + col * 4 + q]).start()
            return carry

        lax.fori_loop(0, 4, rows_of, 0)
    for col in range(2):
        for q in range(4):
            span = pl.ds(q * 128, 128)
            pltpu.make_async_copy(out.at[col, :, span], out_hbm.at[col, :, span], sem.at[1 + col * 4 + q]).wait()
    grid_copy.wait()


def place(offsets, column_index, subgrid_offsets, here, gathered, grids):
    smem = pl.BlockSpec(memory_space=pltpu.SMEM)
    hbm = pl.BlockSpec(memory_space=pltpu.HBM)
    vmem = pl.BlockSpec(memory_space=pltpu.VMEM)
    gathered = pltpu.with_memory_space_constraint(gathered, pltpu.VMEM)
    grids = pltpu.with_memory_space_constraint(grids, pltpu.VMEM)
    return pl.pallas_call(
        place_kernel,
        out_shape=(
            jax.ShapeDtypeStruct((2, 2, XM, SHARD), BF16),
            jax.ShapeDtypeStruct((2, 2, 32, XM), BF16),
        ),
        in_specs=[smem, smem, smem, smem, vmem, vmem],
        out_specs=(hbm, hbm),
        scratch_shapes=[
            pltpu.VMEM((2, 2, XM, SHARD), BF16),
            pltpu.SemaphoreType.DMA((9,)),
        ],
        compiler_params=pltpu.CompilerParams(vmem_limit_bytes=16 << 20),
        name="place",
    )(offsets, column_index, subgrid_offsets, here, gathered, grids)


def per_device(facet_spectra, facet_offsets, column_index, subgrid_offsets, weights):
    spectra = facet_spectra.reshape(2, 2, XM, SHARD)
    subgrid_offsets = subgrid_offsets.reshape(2)
    grids, gathered = exchange(
        facet_offsets, column_index, subgrid_offsets, spectra, weights.reshape(2, 32, XM)
    )
    here = lax.axis_index("col").astype(I32).reshape(1)
    updates, grids = place(facet_offsets, column_index, subgrid_offsets, here, gathered, grids)
    return grids.reshape(2, 1, 2, 32, XM), updates.reshape(2, 1, 2, XM, SHARD)


def solution(mesh):
    in_specs = (
        P(None, "facet", None, None, "col"),
        P("facet", None),
        P(),
        P(None, "col"),
        P(None, "col", "facet", None),
    )
    out_specs = (P(None, "col", None, "facet", None), P(None, "facet", None, None, "col"))
    return jax.shard_map(
        per_device, mesh=mesh, in_specs=in_specs, out_specs=out_specs, check_vma=False
    )
```

time: 46.1 us -> 39.8 us (0.86)
  Pallas kernels: 45.3 us -> 39 us
    pallas_call x2, Pallas kernels: 45.3 us -> 39 us  [the longest x1 35.7 us: exchange(): pl.pallas_call(exchange_kernel, out_shape=(pltpu.VMEM((2, 2, 32, XM), BF1...]
where the time goes in v3:
time: 39.8 us; the launch traced here: 39.7 us
  Pallas kernels  39 us (98%)
  between operations  0.69 us (2%)
    pallas_call x1, Pallas kernels, exchange(): pl.pallas_call(exchange_kernel, out_shape=(pltpu.VMEM((2, 2, 32, XM), BF1...  35.7 us
    pallas_call x1, Pallas kernels, place(): pl.pallas_call(place_kernel, out_shape=(jax.ShapeDtypeStruct((2, 2, XM, S...  3.27 us

profile of v3, /device:TPU:1, one launch (start us, length us, event | category | flops | bytes accessed | tf_op | source)
XLA Modules:
  0.0 39.7 jit_solution(5149460496422159057)
XLA Ops:
  0.6 0.0 copy-start.1
  0.6 0.0 copy-start
  0.7 0.0 copy-start.2
  0.7 35.7 %exchange.1 = (bf16[2,2,32,512]{3,2,1,0:T(8,128)(2,1)S(1)}, bf16[2,2,4,2,128,128]{5,4,3,2,1,0:T(8,128)(2,1)S(1)}) custom-call(s32[1,2]{1,0:T(1,128)} %offs_ref.1, s32[2]{0:T(128)} %colidx_ref.1, s32[2]{0:T(128)} %bitcast.10, bf16[2,2,512,1024]{3,2,1,0:T(8,128)(2,1)} %bitcast.12, bf16[2,32,512]{2,1,0:T(8,128)(2,1)} %bitcast.13, ...), custom_call_target="tpu_custom_call" | custom-call | tf_op jit(solution)/shard_map/exchange/pallas_call | solution.py:324
  36.4 0.0 copy-done.1
  36.4 0.0 copy-done
  36.4 0.0 copy-done.2
  36.4 3.3 %place.1 = (bf16[2,2,512,1024]{3,2,1,0:T(8,128)(2,1)}, bf16[2,2,32,512]{3,2,1,0:T(8,128)(2,1)}) custom-call(s32[1,2]{1,0:T(1,128)S(1)} %copy-done, s32[2]{0:T(128)S(1)} %copy-done.1, s32[2]{0:T(128)S(1)} %bitcast.11, s32[1]{0:T(128)} %bitcast.1.here_ref, bf16[2,2,4,2,128,128]{5,4,3,2,1,0:T(8,128)(2,1)S(1)} %get-tuple-element.6.u_ref, ...), custom_call_target="tpu_custom_call" | custom-call | tf_op jit(solution)/shard_map/place/pallas_call | solution.py:421
Async XLA Ops:
  0.6 35.7 %copy-start.1 = (s32[2]{0:T(128)S(1)}, s32[2]{0:T(128)}, u32[]{:S(2)}) copy-start(s32[2]{0:T(128)} %colidx_ref.1) | copy-start | bytes 28
  0.6 35.7 %copy-start = (s32[1,2]{1,0:T(1,128)S(1)}, s32[1,2]{1,0:T(1,128)}, u32[]{:S(2)}) copy-start(s32[1,2]{1,0:T(1,128)} %offs_ref.1) | copy-start | bytes 28
  0.7 35.7 %copy-start.2 = (s32[2,1]{0,1:T(1,128)S(1)}, s32[2,1]{0,1:T(1,128)}, u32[]{:S(2)}) copy-start(s32[2,1]{0,1:T(1,128)} %param.10) | copy-start | bytes 28

commit v4 on v3

--- a/solution.py
+++ b/solution.py
@@ -65,7 +65,7 @@
 def exchange_kernel(
     offs_hbm, colidx_hbm, sub_hbm, x_hbm, w_hbm, t_hbm, tt_hbm,
     grid_out, g,
-    offs_ref, colidx_ref, sub_ref, x_v, w_v, t_v, tt_v, y, r1, rx, s2, r3, above, below, eo,
+    offs_ref, colidx_ref, sub_ref, x_v, w_v, t_v, tt_v, y, r1, rx, s2, rz, eo,
     grid_v, local_sem, ss, rs,
 ):
     f = lax.axis_index("facet")
@@ -98,11 +98,20 @@
         pl.semaphore_signal(barrier, inc=1, device_id=peer, device_id_type=MESH)
 
     loads = [
-        pltpu.make_async_copy(x_hbm.at[0], x_v.at[0], local_sem.at[0]),
-        pltpu.make_async_copy(x_hbm.at[1], x_v.at[1], local_sem.at[1]),
         pltpu.make_async_copy(t_hbm, t_v, local_sem.at[2]),
         pltpu.make_async_copy(tt_hbm, tt_v, local_sem.at[3]),
         pltpu.make_async_copy(w_hbm, w_v.at[zh], local_sem.at[4]),
+    ]
+    spectra = [
+        [
+            pltpu.make_async_copy(
+                x_hbm.at[col, part, pl.ds(256 * half, 256)],
+                x_v.at[col, part, pl.ds(256 * half, 256)],
+                local_sem.at[col],
+            )
+            for half in range(2) for part in range(2)
+        ]
+        for col in range(2)
     ]
     scalars = [
         pltpu.make_async_copy(source, target, local_sem.at[6 + index])
@@ -112,19 +121,26 @@
     ]
     for load in scalars:
         load.start()
-    loads[0].start()
-
-    sends = []
-
-    def send(src, dst, f_to, c_to=None):
-        index = len(sends)
-        copy = pltpu.make_async_remote_copy(
-            src_ref=src, dst_ref=dst, send_sem=ss.at[index], recv_sem=rs.at[index],
+    for load in spectra[0]:
+        load.start()
+
+    used = []
+
+    def group():
+        used.append(None)
+        return rs.at[len(used) - 1]
+
+    sent = []
+
+    def send(src, dst, arrived, f_to, c_to=None):
+        sent.append(math.prod(src.shape))
+        pltpu.make_async_remote_copy(
+            src_ref=src, dst_ref=dst, send_sem=ss.at[0], recv_sem=arrived,
             device_id=(f_to, c if c_to is None else c_to), device_id_type=MESH,
-        )
-        copy.start()
-        sends.append(copy)
-        return copy
+        ).start()
+
+    def arrive(whole, arrived):
+        pltpu.make_async_copy(whole, whole, arrived).wait()
 
     for load in scalars:
         load.wait()
@@ -148,8 +164,8 @@
         bits = [(jnp.full((128, 128), 0, I32) + tile) & (1 << bit) != 0 for bit in range(3)]
         wide = iota((128, 128), 1) < HALF
 
-        def rows(q, carry):
-            span = pl.ds(pl.multiple_of(q * 128, 128), 128)
+        for q in range(4):
+            span = pl.ds(q * 128, 128)
             pairs = []
             for part in range(2):
                 tiles = [x_v[col, part, span, 128 * i:128 * i + 128] for i in range(8)]
@@ -180,9 +196,6 @@
                 block[80:96] = jnp.where(lane < HALF, e_im[a:b], swap_im[b:d]).astype(BF16)
                 block[96:112] = jnp.where(lane < HALF, swap_re[a:b], e_re[b:d]).astype(BF16)
                 block[112:128] = jnp.where(lane < HALF, swap_im[a:b], e_im[b:d]).astype(BF16)
-            return carry
-
-        lax.fori_loop(0, 4, rows, 0)
 
     def total(*refs):
         result = refs[0][...].astype(F32)
@@ -191,48 +204,48 @@
         return result
 
     order = (2, 1, 3, 0)
-    to_core = []
-    weights_there = None
-    for col in range(2):
-        loads[col].wait()
-        for load in loads[1:2] if col == 0 else loads[2:]:
+    from_core = [group() for _ in range(2)]
+    from_z_weights = group()
+    for col in range(2):
+        arrive(x_v.at[col], local_sem.at[col])
+        for load in spectra[1] if col == 0 else loads:
             load.start()
         phased(col)
         if col == 0:
             pl.semaphore_wait(barrier, len(peers))
-        to_core.append([send(y.at[col, 1 - core, x_of(d)], r1.at[col, x_of(d)], f_core) for d in order])
-        if col == 0:
-            weights_there = send(w_hbm, w_v.at[zh], f_z)
-
-    to_x = []
-    for col in range(2):
-        copies = []
-        for d, copy in zip(order, to_core[col]):
-            copy.wait_recv()
+        send(y.at[col, 1 - core], r1.at[col], from_core[col], f_core)
+    send(w_hbm, w_v.at[zh], from_z_weights, f_z)
+
+    from_x = [group() for _ in range(2)]
+    for col in range(2):
+        arrive(r1.at[col], from_core[col])
+        for d in order[:3]:
             xx = x_of(d)
-            if d:
-                y[col, core, xx] = total(y.at[col, core, xx], r1.at[col, xx]).astype(BF16)
-                copies.append(send(y.at[col, core, xx], rx.at[col, d - 1], f_x[d]))
-        to_x.append(copies)
-
-    to_z = []
-    for col in range(2):
-        for copy in to_x[col]:
-            copy.wait_recv()
+            y[col, core, xx] = total(y.at[col, core, xx], r1.at[col, xx]).astype(BF16)
+            send(y.at[col, core, xx], rx.at[col, d - 1], from_x[col], f_x[d])
+
+    from_z = [group() for _ in range(2)]
+    for col in range(2):
+        arrive(rx.at[col], from_x[col])
         s2[col] = total(
             y.at[col, core, x], r1.at[col, x], rx.at[col, 0], rx.at[col, 1], rx.at[col, 2]
         ).astype(BF16)
-        copies = [send(s2.at[col, :, pl.ds(0, 64)], r3.at[col], f_z)]
-        for k, f_to in enumerate((f, f_z)):
-            copies.append(send(s2.at[col, :, pl.ds(64, 32)], above.at[col, k], f_to, c_prev))
-            copies.append(send(s2.at[col, :, pl.ds(96, 32)], below.at[col, k], f_to, c_next))
-        to_z.append(copies)
-
-    for load in loads[2:]:
+        send(s2.at[col, :, pl.ds(0, 64)], rz.at[col, pl.ds(4, 2)], from_z[col], f_z)
+        for k, f_to in enumerate((f_z, f)):
+            for side, c_to in enumerate((c_next, c_prev)):
+                send(
+                    s2.at[col, :, pl.ds(96 - 32 * side, 32)],
+                    rz.at[col, pl.ds(2 * side, 2), pl.ds(32 * k, 32)],
+                    from_z[col], f_to, c_to,
+                )
+
+    for load in loads:
         load.wait()
-    weights_there.wait_recv()
-
-    to_all = []
+    arrive(w_v.at[1 - zh], from_z_weights)
+
+    from_mains = [[group() for _ in range(3)] for _ in range(2)]
+    from_edges = [[group() for _ in range(4)] for _ in range(2)]
+    passed = [[group() for _ in range(2)] for _ in range(2)]
     for col in range(2):
         start = starts[col]
 
@@ -244,11 +257,14 @@
         side0, side1 = iota((256, 256), 0), iota((256, 256), 1)
         gather_in = matrix(side0, side1)
         gather_out = matrix(side1, side0)
-        for copy in to_z[col]:
-            copy.wait_recv()
-        main = total(s2.at[col, :, pl.ds(0, 64)], r3.at[col])
-        low = total(below.at[col, 0], below.at[col, 1]).reshape(64, 128)
-        high = total(above.at[col, 0], above.at[col, 1]).reshape(64, 128)
+        arrive(rz.at[col], from_z[col])
+        main = total(s2.at[col, :, pl.ds(0, 64)], rz.at[col, pl.ds(4, 2)])
+        low, high = (
+            total(
+                rz.at[col, pl.ds(2 * side, 2), pl.ds(0, 32)], rz.at[col, pl.ds(2 * side, 2), pl.ds(32, 32)]
+            ).reshape(64, 128)
+            for side in range(2)
+        )
         edge = dot(jnp.concatenate([low, high], axis=1).astype(BF16), gather_in)
         windows = []
         for part in range(2):
@@ -281,40 +297,37 @@
         eo[col, 0] = out_edge[:, 0:128].reshape(2, 32, 128)
         eo[col, 1] = out_edge[:, 128:256].reshape(2, 32, 128)
         low, high = g.at[col, :, x, core, pl.ds(64, 32)], g.at[col, :, x, core, pl.ds(96, 32)]
-        edges = []
         for d in order:
-            edges.append((
-                send(eo.at[col, 0], high, facet(zh_prev, x_of(d), core), c_prev),
-                send(eo.at[col, 1], low, facet(zh_next, x_of(d), core), c_next),
-            ))
+            send(eo.at[col, 0], high, from_edges[col][d], facet(zh_prev, x_of(d), core), c_prev)
+            send(eo.at[col, 1], low, from_edges[col][d], facet(zh_next, x_of(d), core), c_next)
         home = g.at[col, :, x, core, pl.ds(0, 64)]
-        mains = [send(home, home, f_x[d]) for d in (2, 1, 3)]
-        to_all.append((mains, edges, [send(home, home, f_core)]))
+        for d in (2, 1, 3):
+            send(home, home, from_mains[col][d - 1], f_x[d])
+        send(home, home, passed[col][0], f_core)
 
     grid_copy = pltpu.make_async_copy(grid_v.at[zh], grid_out, local_sem.at[5])
     grid_copy.start()
 
     for col in range(2):
-        mains, edges, passed = to_all[col]
-        for d, copy in ((1, mains[1]), (3, mains[2]), (2, mains[0])):
-            copy.wait_recv()
+        for d in (1, 3, 2):
             block = g.at[col, :, x_of(4 - d), core, pl.ds(0, 64)]
-            passed.append(send(block, block, f_core))
-        for d, pair in zip(order, edges):
-            for copy in pair:
-                copy.wait_recv()
+            arrive(block, from_mains[col][d - 1])
+            send(block, block, passed[col][0], f_core)
+        for d in order:
             block = g.at[col, :, x_of(4 - d), core, pl.ds(64, 64)]
-            passed.append(send(block, block, f_core))
-    for col in range(2):
-        for copy in to_all[col][2]:
-            copy.wait_recv()
-
-    for copy in sends:
-        copy.wait_send()
+            arrive(block, from_edges[col][d])
+            send(block, block, passed[col][1], f_core)
+    for col in range(2):
+        for half in range(2):
+            arrive(g.at[col, :, :, 1 - core, pl.ds(64 * half, 64)], passed[col][half])
+
+    assert len(used) == N_GROUPS
+    every = sum(sent) // SHARD
+    arrive(x_v.reshape(2 * 2 * XM, SHARD).at[pl.ds(0, every)], ss.at[0])
     grid_copy.wait()
 
 
-N_SENDS = 63
+N_GROUPS = 25
 
 
 def exchange(offsets, column_index, subgrid_offsets, spectra, weights):
@@ -341,24 +354,34 @@
             pltpu.VMEM((2, 4, 2, 128, 128), BF16),
             pltpu.VMEM((2, 3, 2, 128, 128), BF16),
             pltpu.VMEM((2, 2, 128, 128), BF16),
-            pltpu.VMEM((2, 2, 64, 128), BF16),
-            pltpu.VMEM((2, 2, 2, 32, 128), BF16),
-            pltpu.VMEM((2, 2, 2, 32, 128), BF16),
+            pltpu.VMEM((2, 6, 64, 128), BF16),
             pltpu.VMEM((2, 2, 2, 32, 128), BF16),
             pltpu.VMEM((2, 2, 2, 32, XM), BF16),
             pltpu.SemaphoreType.DMA((9,)),
-            pltpu.SemaphoreType.DMA((N_SENDS,)),
-            pltpu.SemaphoreType.DMA((N_SENDS,)),
+            pltpu.SemaphoreType.DMA((1,)),
+            pltpu.SemaphoreType.DMA((N_GROUPS,)),
         ],
         compiler_params=pltpu.CompilerParams(collective_id=0, has_side_effects=True),
         name="exchange",
     )(offsets, column_index, subgrid_offsets, spectra, weights, jnp.asarray(table), jnp.asarray(table_t))
 
 
-def place_kernel(offs_ref, colidx_ref, sub_ref, here_ref, u_ref, grid_ref, out_hbm, grid_hbm, out, sem):
+def place_kernel(offs_hbm, colidx_hbm, sub_hbm, u_ref, grid_ref, out_hbm, grid_hbm, offs_ref, colidx_ref, sub_ref, out, sem):
     grid_copy = pltpu.make_async_copy(grid_ref, grid_hbm, sem.at[0])
     grid_copy.start()
-    c = here_ref[0]
+    scalars = [
+        pltpu.make_async_copy(source, target, sem.at[9 + index])
+        for index, (source, target) in enumerate(
+            ((offs_hbm, offs_ref), (colidx_hbm, colidx_ref), (sub_hbm, sub_ref))
+        )
+    ]
+    for load in scalars:
+        load.start()
+    for col in range(2):
+        out[col] = jnp.zeros((2, XM, SHARD), BF16)
+    for load in scalars:
+        load.wait()
+    c = lax.axis_index("col")
     first, second = offs_ref[0, 0], offs_ref[0, 1]
     spot = iota((8, 128), 1)
     spot = c * SHARD + jnp.where(spot < HALF, spot, SHARD - 128 + spot)
@@ -375,12 +398,13 @@
         put = (iota((128, 256), 1) + base == iota((128, 256), 0) + start).astype(F32).astype(BF16)
         tiles = pl.ds(pl.multiple_of(base, 128), 256)
 
-        def rows_of(q, carry):
-            span = pl.ds(pl.multiple_of(q * 128, 128), 128)
-            out[col, :, span] = jnp.zeros((2, 128, SHARD), BF16)
+        for q in range(4):
+            span = pl.ds(q * 128, 128)
+            some = u_ref.at[col, q // 2, pl.ds((q % 2) * 2, 2)]
+            moved = dot(some[:, :, 0:64].reshape(256, 128), put)
             for j in range(4):
-                block = u_ref.at[col, q // 2, (q % 2) * 2 + j // 2, j % 2]
-                rows = pl.ds(pl.multiple_of(q * 128 + 32 * j, 32), 32)
+                block = some.at[j // 2, j % 2]
+                rows = pl.ds(q * 128 + 32 * j, 32)
                 low_re, low_im = block[64:80].astype(F32), block[80:96].astype(F32)
                 top_re, top_im = block[96:112].astype(F32), block[112:128].astype(F32)
                 edges = []
@@ -395,16 +419,13 @@
                 for part, edge in ((0, edge_re), (1, edge_im)):
                     out[col, part, rows, 0:128] = jnp.where(wide, edge, zero).astype(BF16)
                     out[col, part, rows, SHARD - 128:SHARD] = jnp.where(wide, zero, edge).astype(BF16)
-                moved = dot(block[0:64], put)
-                main_re, main_im = moved[0:32], moved[32:64]
+                main_re, main_im = moved[64 * j:64 * j + 32], moved[64 * j + 32:64 * j + 64]
                 out_re = main_re * cosine - main_im * sine
                 out_im = main_im * cosine + main_re * sine
                 for part, value in ((0, out_re), (1, out_im)):
                     out[col, part, rows, tiles] = (out[col, part, rows, tiles].astype(F32) + value).astype(BF16)
             pltpu.make_async_copy(out.at[col, :, span], out_hbm.at[col, :, span], sem.at[1 + col * 4 + q]).start()
-            return carry
-
-        lax.fori_loop(0, 4, rows_of, 0)
+
     for col in range(2):
         for q in range(4):
             span = pl.ds(q * 128, 128)
@@ -412,8 +433,7 @@
     grid_copy.wait()
 
 
-def place(offsets, column_index, subgrid_offsets, here, gathered, grids):
-    smem = pl.BlockSpec(memory_space=pltpu.SMEM)
+def place(offsets, column_index, subgrid_offsets, gathered, grids):
     hbm = pl.BlockSpec(memory_space=pltpu.HBM)
     vmem = pl.BlockSpec(memory_space=pltpu.VMEM)
     gathered = pltpu.with_memory_space_constraint(gathered, pltpu.VMEM)
@@ -424,15 +444,18 @@
             jax.ShapeDtypeStruct((2, 2, XM, SHARD), BF16),
             jax.ShapeDtypeStruct((2, 2, 32, XM), BF16),
         ),
-        in_specs=[smem, smem, smem, smem, vmem, vmem],
+        in_specs=[hbm, hbm, hbm, vmem, vmem],
         out_specs=(hbm, hbm),
         scratch_shapes=[
+            pltpu.SMEM((1, 2), I32),
+            pltpu.SMEM((2,), I32),
+            pltpu.SMEM((2,), I32),
             pltpu.VMEM((2, 2, XM, SHARD), BF16),
-            pltpu.SemaphoreType.DMA((9,)),
+            pltpu.SemaphoreType.DMA((12,)),
         ],
         compiler_params=pltpu.CompilerParams(vmem_limit_bytes=16 << 20),
         name="place",
-    )(offsets, column_index, subgrid_offsets, here, gathered, grids)
+    )(offsets, column_index, subgrid_offsets, gathered, grids)
 
 
 def per_device(facet_spectra, facet_offsets, column_index, subgrid_offsets, weights):
@@ -441,8 +464,7 @@
     grids, gathered = exchange(
         facet_offsets, column_index, subgrid_offsets, spectra, weights.reshape(2, 32, XM)
     )
-    here = lax.axis_index("col").astype(I32).reshape(1)
-    updates, grids = place(facet_offsets, column_index, subgrid_offsets, here, gathered, grids)
+    updates, grids = place(facet_offsets, column_index, subgrid_offsets, gathered, grids)
     return grids.reshape(2, 1, 2, 32, XM), updates.reshape(2, 1, 2, XM, SHARD)
 
 

time: 39.8 us -> 38.9 us (0.977)
  Pallas kernels: 39 us -> 38 us
    pallas_call x1, Pallas kernels: 35.7 us -> 35.1 us  [exchange(): pl.pallas_call(exchange_kernel, out_shape=(pltpu.VMEM((2, 2, 32, XM), BF1...]
where the time goes in v4:
time: 38.9 us; the launch traced here: 38.7 us
  Pallas kernels  38 us (98%)
  between operations  0.69 us (2%)
    pallas_call x1, Pallas kernels, exchange(): pl.pallas_call(exchange_kernel, out_shape=(pltpu.VMEM((2, 2, 32, XM), BF1...  35.1 us
    pallas_call x1, Pallas kernels, place(): pl.pallas_call(place_kernel, out_shape=(jax.ShapeDtypeStruct((2, 2, XM, S...  2.94 us

profile of v4, /device:TPU:1, one launch (start us, length us, event | category | flops | bytes accessed | tf_op | source)
XLA Modules:
  0.0 38.7 jit_solution(10689413703926884152)
XLA Ops:
  0.6 0.0 copy-start.1
  0.6 0.0 copy-start
  0.7 0.0 copy-start.2
  0.7 35.1 %exchange.1 = (bf16[2,2,32,512]{3,2,1,0:T(8,128)(2,1)S(1)}, bf16[2,2,4,2,128,128]{5,4,3,2,1,0:T(8,128)(2,1)S(1)}) custom-call(s32[1,2]{1,0:T(1,128)} %offs_hbm.3, s32[2]{0:T(128)} %colidx_hbm.3, s32[2]{0:T(128)} %bitcast.9, bf16[2,2,512,1024]{3,2,1,0:T(8,128)(2,1)} %bitcast.11, bf16[2,32,512]{2,1,0:T(8,128)(2,1)} %bitcast.12, ...), custom_call_target="tpu_custom_call" | custom-call | tf_op jit(solution)/shard_map/exchange/pallas_call | solution.py:337
  35.8 0.0 copy-done.1
  35.8 0.0 copy-done
  35.8 0.0 copy-done.2
  35.8 2.9 %place.1 = (bf16[2,2,512,1024]{3,2,1,0:T(8,128)(2,1)}, bf16[2,2,32,512]{3,2,1,0:T(8,128)(2,1)}) custom-call(s32[1,2]{1,0:T(1,128)S(1)} %copy-done, s32[2]{0:T(128)S(1)} %copy-done.1, s32[2]{0:T(128)S(1)} %bitcast.10, bf16[2,2,4,2,128,128]{5,4,3,2,1,0:T(8,128)(2,1)S(1)} %get-tuple-element.6.u_ref, bf16[2,2,32,512]{3,2,1,0:T(8,128)(2,1)S(1)} %get-tuple-element.7.grid_ref), custom_call_target="tpu_custom_call" | custom-call | tf_op jit(solution)/shard_map/place/pallas_call | solution.py:441
Async XLA Ops:
  0.6 35.1 %copy-start.1 = (s32[2]{0:T(128)S(1)}, s32[2]{0:T(128)}, u32[]{:S(2)}) copy-start(s32[2]{0:T(128)} %colidx_hbm.3) | copy-start | bytes 28
  0.6 35.1 %copy-start = (s32[1,2]{1,0:T(1,128)S(1)}, s32[1,2]{1,0:T(1,128)}, u32[]{:S(2)}) copy-start(s32[1,2]{1,0:T(1,128)} %offs_hbm.3) | copy-start | bytes 28
  0.7 35.1 %copy-start.2 = (s32[2,1]{0,1:T(1,128)S(1)}, s32[2,1]{0,1:T(1,128)}, u32[]{:S(2)}) copy-start(s32[2,1]{0,1:T(1,128)} %param.10) | copy-start | bytes 28

commit v5 on v4

--- a/solution.py
+++ b/solution.py
@@ -65,7 +65,7 @@
 def exchange_kernel(
     offs_hbm, colidx_hbm, sub_hbm, x_hbm, w_hbm, t_hbm, tt_hbm,
     grid_out, g,
-    offs_ref, colidx_ref, sub_ref, x_v, w_v, t_v, tt_v, y, r1, rx, s2, rz, eo,
+    offs_ref, colidx_ref, sub_ref, x_v, w_v, t_v, tt_v, y, r1, rx, ex, s2, rz, eo,
     grid_v, local_sem, ss, rs,
 ):
     f = lax.axis_index("facet")
@@ -91,9 +91,8 @@
 
     barrier = pltpu.get_barrier_semaphore()
     peers = [(f_core, c), (f_z, c), (f_x[1], c), (f_x[2], c), (f_x[3], c)]
-    peers += [(f, c_prev), (f_z, c_prev), (f, c_next), (f_z, c_next)]
-    peers += [(facet(zh_prev, x_of(d), core), c_prev) for d in (1, 2, 3)]
-    peers += [(facet(zh_next, x_of(d), core), c_next) for d in (1, 2, 3)]
+    peers += [(facet(zh_prev, x_of(d), core), c_prev) for d in range(4)]
+    peers += [(facet(zh_next, x_of(d), core), c_next) for d in range(4)]
     for peer in peers:
         pl.semaphore_signal(barrier, inc=1, device_id=peer, device_id_type=MESH)
 
@@ -144,6 +143,8 @@
 
     for load in scalars:
         load.wait()
+    for load in spectra[1]:
+        load.start()
     lane = iota((16, 128), 1)
     first, second = offs_ref[0, 0], offs_ref[0, 1]
     starts = []
@@ -208,8 +209,9 @@
     from_z_weights = group()
     for col in range(2):
         arrive(x_v.at[col], local_sem.at[col])
-        for load in spectra[1] if col == 0 else loads:
-            load.start()
+        if col == 1:
+            for load in loads:
+                load.start()
         phased(col)
         if col == 0:
             pl.semaphore_wait(barrier, len(peers))
@@ -217,27 +219,41 @@
     send(w_hbm, w_v.at[zh], from_z_weights, f_z)
 
     from_x = [group() for _ in range(2)]
+    from_near = [group() for _ in range(2)]
     for col in range(2):
         arrive(r1.at[col], from_core[col])
-        for d in order[:3]:
+        for d in order:
             xx = x_of(d)
             y[col, core, xx] = total(y.at[col, core, xx], r1.at[col, xx]).astype(BF16)
-            send(y.at[col, core, xx], rx.at[col, d - 1], from_x[col], f_x[d])
+            block = y.at[col, core, xx]
+            send(block.at[:, pl.ds(64, 32)], ex.at[col, 1, d], from_near[col], facet(zh_prev, xx, core), c_prev)
+            send(block.at[:, pl.ds(96, 32)], ex.at[col, 0, d], from_near[col], facet(zh_next, xx, core), c_next)
+            if d:
+                send(block.at[:, pl.ds(0, 64)], rx.at[col, d - 1], from_x[col], f_x[d])
+
+    def matrix(source, window, start):
+        cell = (source & 63) + jnp.where(source < 128, -HALF, SHARD) - start
+        same = (lax.shift_right_logical(source, 6) & 1) == lax.shift_right_logical(window, 7)
+        return jnp.where(same & (cell == (window & 127)), 1.0, 0.0).astype(BF16)
+
+    side0, side1 = iota((256, 256), 0), iota((256, 256), 1)
+    gather_in = [matrix(side0, side1, start) for start in starts]
+    gather_out = [matrix(side1, side0, start) for start in starts]
 
     from_z = [group() for _ in range(2)]
     for col in range(2):
         arrive(rx.at[col], from_x[col])
-        s2[col] = total(
-            y.at[col, core, x], r1.at[col, x], rx.at[col, 0], rx.at[col, 1], rx.at[col, 2]
-        ).astype(BF16)
-        send(s2.at[col, :, pl.ds(0, 64)], rz.at[col, pl.ds(4, 2)], from_z[col], f_z)
-        for k, f_to in enumerate((f_z, f)):
-            for side, c_to in enumerate((c_next, c_prev)):
-                send(
-                    s2.at[col, :, pl.ds(96 - 32 * side, 32)],
-                    rz.at[col, pl.ds(2 * side, 2), pl.ds(32 * k, 32)],
-                    from_z[col], f_to, c_to,
-                )
+        main = total(y.at[col, core, x, :, pl.ds(0, 64)], rx.at[col, 0], rx.at[col, 1], rx.at[col, 2])
+        arrive(ex.at[col], from_near[col])
+        low, high = (total(*(ex.at[col, side, d] for d in range(4))).reshape(64, 128) for side in range(2))
+        edge = dot(jnp.concatenate([low, high], axis=1).astype(BF16), gather_in[col])
+        for half in range(2):
+            for part in range(2):
+                a = half * 32 + part * 16
+                reach = jnp.concatenate([edge[a:a + 16, 0:128], edge[a:a + 16, 128:256]], axis=0)
+                rows = slice(part * 32, part * 32 + 32)
+                s2[col, half, rows] = (main[half, rows] + reach).astype(BF16)
+        send(s2.at[col], rz.at[col], from_z[col], f_z)
 
     for load in loads:
         load.wait()
@@ -247,32 +263,11 @@
     from_edges = [[group() for _ in range(4)] for _ in range(2)]
     passed = [[group() for _ in range(2)] for _ in range(2)]
     for col in range(2):
-        start = starts[col]
-
-        def matrix(source, window):
-            cell = (source & 63) + jnp.where(source < 128, -HALF, SHARD) - start
-            same = (lax.shift_right_logical(source, 6) & 1) == lax.shift_right_logical(window, 7)
-            return jnp.where(same & (cell == (window & 127)), 1.0, 0.0).astype(BF16)
-
-        side0, side1 = iota((256, 256), 0), iota((256, 256), 1)
-        gather_in = matrix(side0, side1)
-        gather_out = matrix(side1, side0)
         arrive(rz.at[col], from_z[col])
-        main = total(s2.at[col, :, pl.ds(0, 64)], rz.at[col, pl.ds(4, 2)])
-        low, high = (
-            total(
-                rz.at[col, pl.ds(2 * side, 2), pl.ds(0, 32)], rz.at[col, pl.ds(2 * side, 2), pl.ds(32, 32)]
-            ).reshape(64, 128)
-            for side in range(2)
-        )
-        edge = dot(jnp.concatenate([low, high], axis=1).astype(BF16), gather_in)
-        windows = []
-        for part in range(2):
-            for half in range(2):
-                a = half * 32 + part * 16
-                reach = jnp.concatenate([edge[a:a + 16, 0:128], edge[a:a + 16, 128:256]], axis=0)
-                windows.append(main[half, part * 32:part * 32 + 32] + reach)
-        window = jnp.concatenate(windows, axis=0).astype(BF16)
+        main = total(s2.at[col], rz.at[col])
+        window = jnp.concatenate(
+            [main[half, part * 32:part * 32 + 32] for part in range(2) for half in range(2)], axis=0
+        ).astype(BF16)
         prod = dot(window, t_v[...])
         cells_re = (prod[0:64, 0:XM] - prod[64:128, XM:2 * XM]).astype(BF16)
         cells_im = (prod[0:64, XM:2 * XM] + prod[64:128, 0:XM]).astype(BF16)
@@ -293,7 +288,7 @@
             block[32:64] = back_im[a:a + 32]
             for back in (back_re, back_im):
                 packed.append(jnp.concatenate([back[a:a + 16], back[a + 16:a + 32]], axis=1))
-        out_edge = dot(jnp.concatenate(packed, axis=0), gather_out).astype(BF16)
+        out_edge = dot(jnp.concatenate(packed, axis=0), gather_out[col]).astype(BF16)
         eo[col, 0] = out_edge[:, 0:128].reshape(2, 32, 128)
         eo[col, 1] = out_edge[:, 128:256].reshape(2, 32, 128)
         low, high = g.at[col, :, x, core, pl.ds(64, 32)], g.at[col, :, x, core, pl.ds(96, 32)]
@@ -327,7 +322,7 @@
     grid_copy.wait()
 
 
-N_GROUPS = 25
+N_GROUPS = 27
 
 
 def exchange(offsets, column_index, subgrid_offsets, spectra, weights):
@@ -352,9 +347,10 @@
             pltpu.VMEM((XM, 2 * WM), BF16),
             pltpu.VMEM((2, 2, 4, 2, 128, 128), BF16),
             pltpu.VMEM((2, 4, 2, 128, 128), BF16),
-            pltpu.VMEM((2, 3, 2, 128, 128), BF16),
-            pltpu.VMEM((2, 2, 128, 128), BF16),
-            pltpu.VMEM((2, 6, 64, 128), BF16),
+            pltpu.VMEM((2, 3, 2, 64, 128), BF16),
+            pltpu.VMEM((2, 2, 4, 2, 32, 128), BF16),
+            pltpu.VMEM((2, 2, 64, 128), BF16),
+            pltpu.VMEM((2, 2, 64, 128), BF16),
             pltpu.VMEM((2, 2, 2, 32, 128), BF16),
             pltpu.VMEM((2, 2, 2, 32, XM), BF16),
             pltpu.SemaphoreType.DMA((9,)),

time: 38.9 us -> 37.7 us (0.969)
  Pallas kernels: 38 us -> 36.9 us
    pallas_call x1, Pallas kernels: 35.1 us -> 34 us  [exchange(): pl.pallas_call(exchange_kernel, out_shape=(pltpu.VMEM((2, 2, 32, XM), BF1...]
where the time goes in v5:
time: 37.7 us; the launch traced here: 37.6 us
  Pallas kernels  36.9 us (98%)
  between operations  0.69 us (2%)
    pallas_call x1, Pallas kernels, exchange(): pl.pallas_call(exchange_kernel, out_shape=(pltpu.VMEM((2, 2, 32, XM), BF1...  34 us
    pallas_call x1, Pallas kernels, place(): pl.pallas_call(place_kernel, out_shape=(jax.ShapeDtypeStruct((2, 2, XM, S...  2.93 us

profile of v5, /device:TPU:1, one launch (start us, length us, event | category | flops | bytes accessed | tf_op | source)
XLA Modules:
  0.0 37.6 jit_solution(5301003174966474767)
XLA Ops:
  0.6 0.0 copy-start.1
  0.6 0.0 copy-start
  0.7 0.0 copy-start.2
  0.7 34.0 %exchange.1 = (bf16[2,2,32,512]{3,2,1,0:T(8,128)(2,1)S(1)}, bf16[2,2,4,2,128,128]{5,4,3,2,1,0:T(8,128)(2,1)S(1)}) custom-call(s32[1,2]{1,0:T(1,128)} %offs_hbm.3, s32[2]{0:T(128)} %colidx_hbm.3, s32[2]{0:T(128)} %bitcast.9, bf16[2,2,512,1024]{3,2,1,0:T(8,128)(2,1)} %bitcast.11, bf16[2,32,512]{2,1,0:T(8,128)(2,1)} %bitcast.12, ...), custom_call_target="tpu_custom_call" | custom-call | tf_op jit(solution)/shard_map/exchange/pallas_call | solution.py:332
  34.7 0.0 copy-done.1
  34.7 0.0 copy-done
  34.7 0.0 copy-done.2
  34.7 2.9 %place.1 = (bf16[2,2,512,1024]{3,2,1,0:T(8,128)(2,1)}, bf16[2,2,32,512]{3,2,1,0:T(8,128)(2,1)}) custom-call(s32[1,2]{1,0:T(1,128)S(1)} %copy-done, s32[2]{0:T(128)S(1)} %copy-done.1, s32[2]{0:T(128)S(1)} %bitcast.10, bf16[2,2,4,2,128,128]{5,4,3,2,1,0:T(8,128)(2,1)S(1)} %get-tuple-element.6.u_ref, bf16[2,2,32,512]{3,2,1,0:T(8,128)(2,1)S(1)} %get-tuple-element.7.grid_ref), custom_call_target="tpu_custom_call" | custom-call | tf_op jit(solution)/shard_map/place/pallas_call | solution.py:437
Async XLA Ops:
  0.6 34.0 %copy-start.1 = (s32[2]{0:T(128)S(1)}, s32[2]{0:T(128)}, u32[]{:S(2)}) copy-start(s32[2]{0:T(128)} %colidx_hbm.3) | copy-start | bytes 28
  0.6 34.0 %copy-start = (s32[1,2]{1,0:T(1,128)S(1)}, s32[1,2]{1,0:T(1,128)}, u32[]{:S(2)}) copy-start(s32[1,2]{1,0:T(1,128)} %offs_hbm.3) | copy-start | bytes 28
  0.7 34.0 %copy-start.2 = (s32[2,1]{0,1:T(1,128)S(1)}, s32[2,1]{0,1:T(1,128)}, u32[]{:S(2)}) copy-start(s32[2,1]{0,1:T(1,128)} %param.10) | copy-start | bytes 28

commit v6 on v5

--- a/solution.py
+++ b/solution.py
@@ -64,7 +64,7 @@
 
 def exchange_kernel(
     offs_hbm, colidx_hbm, sub_hbm, x_hbm, w_hbm, t_hbm, tt_hbm,
-    grid_out, g,
+    grid_out, g, info,
     offs_ref, colidx_ref, sub_ref, x_v, w_v, t_v, tt_v, y, r1, rx, ex, s2, rz, eo,
     grid_v, local_sem, ss, rs,
 ):
@@ -151,7 +151,7 @@
     for col in range(2):
         starts.append(lax.shift_right_arithmetic(sub_ref[col], 2) - c * SHARD - HALF)
 
-    def phased(col):
+    def prepared(col):
         start = starts[col]
         column_pos = colidx_ref[col] * XA
         cosine, sine = phase(turns(column_pos, first, second, c * SHARD + start + iota((8, 128), 1)))
@@ -163,8 +163,11 @@
         tile = jnp.clip(lax.shift_right_arithmetic(start, 7), 0, SHARD // 128 - 2)
         pick = (iota((256, 128), 0) + tile * 128 == iota((256, 128), 1) + start).astype(F32).astype(BF16)
         bits = [(jnp.full((128, 128), 0, I32) + tile) & (1 << bit) != 0 for bit in range(3)]
-        wide = iota((128, 128), 1) < HALF
-
+        return cosine, sine, cosine_e, sine_e, pick, bits
+
+    wide = iota((128, 128), 1) < HALF
+
+    def phased(col, cosine, sine, cosine_e, sine_e, pick, bits):
         for q in range(4):
             span = pl.ds(q * 128, 128)
             pairs = []
@@ -207,12 +210,19 @@
     order = (2, 1, 3, 0)
     from_core = [group() for _ in range(2)]
     from_z_weights = group()
+    ready = [prepared(col) for col in range(2)]
+    row = iota((8, 128), 0)
+    known = [starts[0], starts[1]] + [(colidx_ref[col] * XA * first) & 65535 for col in range(2)] + [second]
+    facts = jnp.zeros((8, 128), I32)
+    for index, value in enumerate(known):
+        facts = jnp.where(row == index, value, facts)
+    info[...] = facts.astype(F32)
     for col in range(2):
         arrive(x_v.at[col], local_sem.at[col])
         if col == 1:
             for load in loads:
                 load.start()
-        phased(col)
+        phased(col, *ready[col])
         if col == 0:
             pl.semaphore_wait(barrier, len(peers))
         send(y.at[col, 1 - core], r1.at[col], from_core[col], f_core)
@@ -277,9 +287,6 @@
         prod = dot(jnp.concatenate([scaled_re, scaled_im], axis=0), tt_v[...])
         back_re = (prod[0:64, 0:WM] + prod[64:128, WM:2 * WM]).astype(BF16)
         back_im = (prod[64:128, 0:WM] - prod[0:64, WM:2 * WM]).astype(BF16)
-        for half in range(2):
-            grid_v[half, col, 0] = cells_re[half * 32:half * 32 + 32]
-            grid_v[half, col, 1] = cells_im[half * 32:half * 32 + 32]
         packed = []
         for half in range(2):
             block = g.at[col, half, x, core]
@@ -288,6 +295,10 @@
             block[32:64] = back_im[a:a + 32]
             for back in (back_re, back_im):
                 packed.append(jnp.concatenate([back[a:a + 16], back[a + 16:a + 32]], axis=1))
+        home = g.at[col, :, x, core, pl.ds(0, 64)]
+        for d in (2, 1, 3):
+            send(home, home, from_mains[col][d - 1], f_x[d])
+        send(home, home, passed[col][0], f_core)
         out_edge = dot(jnp.concatenate(packed, axis=0), gather_out[col]).astype(BF16)
         eo[col, 0] = out_edge[:, 0:128].reshape(2, 32, 128)
         eo[col, 1] = out_edge[:, 128:256].reshape(2, 32, 128)
@@ -295,13 +306,9 @@
         for d in order:
             send(eo.at[col, 0], high, from_edges[col][d], facet(zh_prev, x_of(d), core), c_prev)
             send(eo.at[col, 1], low, from_edges[col][d], facet(zh_next, x_of(d), core), c_next)
-        home = g.at[col, :, x, core, pl.ds(0, 64)]
-        for d in (2, 1, 3):
-            send(home, home, from_mains[col][d - 1], f_x[d])
-        send(home, home, passed[col][0], f_core)
-
-    grid_copy = pltpu.make_async_copy(grid_v.at[zh], grid_out, local_sem.at[5])
-    grid_copy.start()
+        for half in range(2):
+            grid_v[half, col, 0] = cells_re[half * 32:half * 32 + 32]
+            grid_v[half, col, 1] = cells_im[half * 32:half * 32 + 32]
 
     for col in range(2):
         for d in (1, 3, 2):
@@ -312,6 +319,8 @@
             block = g.at[col, :, x_of(4 - d), core, pl.ds(64, 64)]
             arrive(block, from_edges[col][d])
             send(block, block, passed[col][1], f_core)
+    grid_copy = pltpu.make_async_copy(grid_v.at[zh], grid_out, local_sem.at[5])
+    grid_copy.start()
     for col in range(2):
         for half in range(2):
             arrive(g.at[col, :, :, 1 - core, pl.ds(64 * half, 64)], passed[col][half])
@@ -334,9 +343,10 @@
         out_shape=(
             pltpu.VMEM((2, 2, 32, XM), BF16),
             pltpu.VMEM((2, 2, 4, 2, 128, 128), BF16),
+            pltpu.VMEM((8, 128), F32),
         ),
         in_specs=[hbm] * 7,
-        out_specs=(vmem, vmem),
+        out_specs=(vmem, vmem, vmem),
         scratch_shapes=[
             pltpu.SMEM((1, 2), I32),
             pltpu.SMEM((2,), I32),
@@ -362,40 +372,29 @@
     )(offsets, column_index, subgrid_offsets, spectra, weights, jnp.asarray(table), jnp.asarray(table_t))
 
 
-def place_kernel(offs_hbm, colidx_hbm, sub_hbm, u_ref, grid_ref, out_hbm, grid_hbm, offs_ref, colidx_ref, sub_ref, out, sem):
+def place_kernel(u_ref, grid_ref, info_ref, out_hbm, grid_hbm, out, sem):
     grid_copy = pltpu.make_async_copy(grid_ref, grid_hbm, sem.at[0])
     grid_copy.start()
-    scalars = [
-        pltpu.make_async_copy(source, target, sem.at[9 + index])
-        for index, (source, target) in enumerate(
-            ((offs_hbm, offs_ref), (colidx_hbm, colidx_ref), (sub_hbm, sub_ref))
-        )
-    ]
-    for load in scalars:
-        load.start()
-    for col in range(2):
-        out[col] = jnp.zeros((2, XM, SHARD), BF16)
-    for load in scalars:
-        load.wait()
+    known = [jnp.max(info_ref[index:index + 1, :]).astype(I32) for index in range(5)]
     c = lax.axis_index("col")
-    first, second = offs_ref[0, 0], offs_ref[0, 1]
+    second = known[4]
     spot = iota((8, 128), 1)
     spot = c * SHARD + jnp.where(spot < HALF, spot, SHARD - 128 + spot)
     lane = iota((16, 128), 1)
     wide = iota((32, 128), 1) < HALF
     for col in range(2):
-        start = lax.shift_right_arithmetic(sub_ref[col], 2) - c * SHARD - HALF
+        start = known[col]
         base = jnp.clip(lax.shift_right_arithmetic(start, 7), 0, SHARD // 128 - 2) * 128
-        column_pos = colidx_ref[col] * XA
-        cosine, sine = phase(turns(column_pos, first, second, c * SHARD + base + iota((8, 256), 1)))
+        cosine, sine = phase(turns(known[2 + col], 1, second, c * SHARD + base + iota((8, 256), 1)))
         cosine, sine = cosine[0:1], sine[0:1]
-        cosine_e, sine_e = phase(turns(column_pos, first, second, spot))
+        cosine_e, sine_e = phase(turns(known[2 + col], 1, second, spot))
         cosine_e, sine_e = cosine_e[0:1], sine_e[0:1]
         put = (iota((128, 256), 1) + base == iota((128, 256), 0) + start).astype(F32).astype(BF16)
         tiles = pl.ds(pl.multiple_of(base, 128), 256)
 
         for q in range(4):
             span = pl.ds(q * 128, 128)
+            out[col, :, span] = jnp.zeros((2, 128, SHARD), BF16)
             some = u_ref.at[col, q // 2, pl.ds((q % 2) * 2, 2)]
             moved = dot(some[:, :, 0:64].reshape(256, 128), put)
             for j in range(4):
@@ -429,38 +428,36 @@
     grid_copy.wait()
 
 
-def place(offsets, column_index, subgrid_offsets, gathered, grids):
+def place(gathered, grids, info):
     hbm = pl.BlockSpec(memory_space=pltpu.HBM)
     vmem = pl.BlockSpec(memory_space=pltpu.VMEM)
     gathered = pltpu.with_memory_space_constraint(gathered, pltpu.VMEM)
     grids = pltpu.with_memory_space_constraint(grids, pltpu.VMEM)
+    info = pltpu.with_memory_space_constraint(info, pltpu.VMEM)
     return pl.pallas_call(
         place_kernel,
         out_shape=(
             jax.ShapeDtypeStruct((2, 2, XM, SHARD), BF16),
             jax.ShapeDtypeStruct((2, 2, 32, XM), BF16),
         ),
-        in_specs=[hbm, hbm, hbm, vmem, vmem],
+        in_specs=[vmem, vmem, vmem],
         out_specs=(hbm, hbm),
         scratch_shapes=[
-            pltpu.SMEM((1, 2), I32),
-            pltpu.SMEM((2,), I32),
-            pltpu.SMEM((2,), I32),
             pltpu.VMEM((2, 2, XM, SHARD), BF16),
-            pltpu.SemaphoreType.DMA((12,)),
+            pltpu.SemaphoreType.DMA((9,)),
         ],
         compiler_params=pltpu.CompilerParams(vmem_limit_bytes=16 << 20),
         name="place",
-    )(offsets, column_index, subgrid_offsets, gathered, grids)
+    )(gathered, grids, info)
 
 
 def per_device(facet_spectra, facet_offsets, column_index, subgrid_offsets, weights):
     spectra = facet_spectra.reshape(2, 2, XM, SHARD)
     subgrid_offsets = subgrid_offsets.reshape(2)
-    grids, gathered = exchange(
+    grids, gathered, info = exchange(
         facet_offsets, column_index, subgrid_offsets, spectra, weights.reshape(2, 32, XM)
     )
-    updates, grids = place(facet_offsets, column_index, subgrid_offsets, gathered, grids)
+    updates, grids = place(gathered, grids, info)
     return grids.reshape(2, 1, 2, 32, XM), updates.reshape(2, 1, 2, XM, SHARD)
 
 

time: 37.7 us -> 37.5 us (level)
  no operation moved by 1% of the time
where the time goes in v6:
time: 37.5 us; the launch traced here: 37.4 us
  Pallas kernels  36.7 us (98%)
  between operations  0.64 us (2%)
    pallas_call x1, Pallas kernels, exchange(): pl.pallas_call(exchange_kernel, out_shape=(pltpu.VMEM((2, 2, 32, XM), BF1...  33.9 us
    pallas_call x1, Pallas kernels, place(): pl.pallas_call(place_kernel, out_shape=(jax.ShapeDtypeStruct((2, 2, XM, S...  2.8 us

profile of v6, /device:TPU:1, one launch (start us, length us, event | category | flops | bytes accessed | tf_op | source)
XLA Modules:
  0.0 37.4 jit_solution(16330686598645121087)
XLA Ops:
  0.6 33.9 %exchange.1 = (bf16[2,2,32,512]{3,2,1,0:T(8,128)(2,1)S(1)}, bf16[2,2,4,2,128,128]{5,4,3,2,1,0:T(8,128)(2,1)S(1)}, f32[8,128]{1,0:T(8,128)S(1)}) custom-call(s32[1,2]{1,0:T(1,128)} %offs_hbm.1, s32[2]{0:T(128)} %colidx_hbm.1, s32[2]{0:T(128)} %bitcast.11, bf16[2,2,512,1024]{3,2,1,0:T(8,128)(2,1)} %bitcast.9, bf16[2,32,512]{2,1,0:T(8,128)(2,1)} %bitcast.10, ...), custom_call_target="tpu_custom_call" | custom-call | tf_op jit(solution)/shard_map/exchange/pallas_call | solution.py:341
  34.5 2.8 %place.1 = (bf16[2,2,512,1024]{3,2,1,0:T(8,128)(2,1)}, bf16[2,2,32,512]{3,2,1,0:T(8,128)(2,1)}) custom-call(bf16[2,2,4,2,128,128]{5,4,3,2,1,0:T(8,128)(2,1)S(1)} %get-tuple-element.7.u_ref, bf16[2,2,32,512]{3,2,1,0:T(8,128)(2,1)S(1)} %get-tuple-element.8.grid_ref, f32[8,128]{1,0:T(8,128)S(1)} %get-tuple-element.9.info_ref), custom_call_target="tpu_custom_call" | custom-call | tf_op jit(solution)/shard_map/place/pallas_call | solution.py:437

commit v7 on v6

--- a/solution.py
+++ b/solution.py
@@ -311,14 +311,11 @@
             grid_v[half, col, 1] = cells_im[half * 32:half * 32 + 32]
 
     for col in range(2):
-        for d in (1, 3, 2):
-            block = g.at[col, :, x_of(4 - d), core, pl.ds(0, 64)]
-            arrive(block, from_mains[col][d - 1])
-            send(block, block, passed[col][0], f_core)
-        for d in order:
-            block = g.at[col, :, x_of(4 - d), core, pl.ds(64, 64)]
-            arrive(block, from_edges[col][d])
-            send(block, block, passed[col][1], f_core)
+        for d, rows in ((1, 0), (3, 0), (2, 64), (1, 64), (3, 64), (0, 64), (2, 0)):
+            block = g.at[col, :, x_of(4 - d), core, pl.ds(rows, 64)]
+            arrive(block, from_edges[col][d] if rows else from_mains[col][d - 1])
+            send(block, block, passed[col][1 if rows else 0], f_core)
+
     grid_copy = pltpu.make_async_copy(grid_v.at[zh], grid_out, local_sem.at[5])
     grid_copy.start()
     for col in range(2):

time: 37.5 us -> 37.5 us (level)
  no operation moved by 1% of the time
where the time goes in v7:
time: 37.5 us; the launch traced here: 37.4 us
  Pallas kernels  36.7 us (98%)
  between operations  0.64 us (2%)
    pallas_call x1, Pallas kernels, exchange(): pl.pallas_call(exchange_kernel, out_shape=(pltpu.VMEM((2, 2, 32, XM), BF1...  33.9 us
    pallas_call x1, Pallas kernels, place(): pl.pallas_call(place_kernel, out_shape=(jax.ShapeDtypeStruct((2, 2, XM, S...  2.8 us

profile of v7, /device:TPU:1, one launch (start us, length us, event | category | flops | bytes accessed | tf_op | source)
XLA Modules:
  0.0 37.4 jit_solution(10301612198882161777)
XLA Ops:
  0.6 33.9 %exchange.1 = (bf16[2,2,32,512]{3,2,1,0:T(8,128)(2,1)S(1)}, bf16[2,2,4,2,128,128]{5,4,3,2,1,0:T(8,128)(2,1)S(1)}, f32[8,128]{1,0:T(8,128)S(1)}) custom-call(s32[1,2]{1,0:T(1,128)} %offs_hbm.1, s32[2]{0:T(128)} %colidx_hbm.1, s32[2]{0:T(128)} %bitcast.11, bf16[2,2,512,1024]{3,2,1,0:T(8,128)(2,1)} %bitcast.9, bf16[2,32,512]{2,1,0:T(8,128)(2,1)} %bitcast.10, ...), custom_call_target="tpu_custom_call" | custom-call | tf_op jit(solution)/shard_map/exchange/pallas_call | solution.py:338
  34.5 2.8 %place.1 = (bf16[2,2,512,1024]{3,2,1,0:T(8,128)(2,1)}, bf16[2,2,32,512]{3,2,1,0:T(8,128)(2,1)}) custom-call(bf16[2,2,4,2,128,128]{5,4,3,2,1,0:T(8,128)(2,1)S(1)} %get-tuple-element.7.u_ref, bf16[2,2,32,512]{3,2,1,0:T(8,128)(2,1)S(1)} %get-tuple-element.8.grid_ref, f32[8,128]{1,0:T(8,128)S(1)} %get-tuple-element.9.info_ref), custom_call_target="tpu_custom_call" | custom-call | tf_op jit(solution)/shard_map/place/pallas_call | solution.py:434
